TPU v7x, 32 devices: a whole 2x2x4 slice. The times are simulated.
32 devices in a mesh: dp: 4 (over z), seq: 8 (over y, x, core).
Axes of the slice: x: 2, y: 2, z: 4, core: 2. Of those that a mesh axis runs over, the one named last changes fastest.
Arguments:
- layer_input: bfloat16 [4, 1024, 2048], P('dp', 'seq'), may hold values from -6 to 6
- document_lengths: int32 [4, 4], P('dp'), may hold values from 1 to 512, 1024 in all within a row
- attention_gain: float32 [2048], replicated, may hold values from 0.5 to 1.5
- attention_in: bfloat16 [2048, 3072], P(('dp', 'seq')), may hold values from -0.125 to 0.125
- query_gain: float32 [64], replicated, may hold values from 0.5 to 1.5
- key_gain: float32 [64], replicated, may hold values from 0.5 to 1.5
- attention_out: bfloat16 [2048, 2048], P(('dp', 'seq')), may hold values from -1 to 1
- feed_gain: float32 [2048], replicated, may hold values from 0.5 to 1.5
- feed_weight: bfloat16 [8192, 6144], P(('dp', 'seq')), may hold values from -0.25 to 0.25
- cotangent: bfloat16 [4, 1024, 2048], P('dp', 'seq'), may hold values from -6 to 6
Outputs:
- layer_output: bfloat16 [4, 1024, 2048], P('dp', 'seq')
- input_gradient: bfloat16 [4, 1024, 2048], P('dp', 'seq')
- attention_gain_gradient: float32 [2048], replicated
- attention_in_gradient: float32 [2048, 3072], P(('dp', 'seq'))
- query_gain_gradient: float32 [64], replicated
- key_gain_gradient: float32 [64], replicated
- attention_out_gradient: float32 [2048, 2048], P(('dp', 'seq'))
- feed_gain_gradient: float32 [2048], replicated
- feed_weight_gradient: float32 [8192, 6144], P(('dp', 'seq'))
Inputs may be any that keep to these rules, and one draw needn't show every extreme that they name: `document_lengths`: each row's 4 document lengths sum to 1024, and the longest of every row is exactly 512.
All inputs are finite; a program needn't handle non-finite values.
Results may differ from a plain program's by a relative error of at most 0.02.
Values may be sent and summed in bfloat16 or wider, within the bound.
No kernel may reach another device: no remote copies, remote signals or barrier semaphores. Data moves between devices by JAX's collectives and lax.ppermute only.
A program may use at most 832 MiB of HBM per device.

v0:
```python
import math

import jax
import jax.numpy as jnp
from jax import lax
from jax.sharding import PartitionSpec as P

D = 2048
HEADS = 32
KV_HEADS = 8
HEAD_DIM = 64


EPSILON = 1e-06
NEGATIVE = -1e30


def shifted(value, axis, steps):
    count = lax.axis_size(axis)
    pairs = [(source, (source + steps) % count) for source in range(count)]
    return lax.ppermute(value, axis, pairs)


def shifted_2(value, axis, steps):
    count = lax.axis_size(axis)
    initial, last = (max(0, -steps), min(count, count - steps))
    return lax.ppermute(value, axis, [(source, source + steps) for source in range(initial, last)])


def normalize(value, gain):
    return value * lax.rsqrt(jnp.mean(value * value, axis=-1, keepdims=True) + EPSILON) * gain


def rotate(value, angles):
    half = value.shape[-1] // 2
    cosine = jnp.cos(angles)[..., None, :]
    sine = jnp.sin(angles)[..., None, :]
    first = value[..., :half]
    second = value[..., half:]
    return jnp.concatenate(
        [first * cosine - second * sine, second * cosine + first * sine], axis=-1
    )


def against(left, right):
    return lax.dot_general(
        left, right, (((1,), (1,)), ((), ())), preferred_element_type=jnp.float32
    )


def across(left, right):
    return lax.dot_general(
        left, right, (((0,), (0,)), ((), ())), preferred_element_type=jnp.float32
    )


def add_rows(left, piece):
    return jnp.dot(left, piece, preferred_element_type=jnp.float32)


def prepare(joined, query_gain, key_gain, angles):
    batch, length = (joined.shape[0], joined.shape[1])
    split_key = D + KV_HEADS * HEAD_DIM
    query = joined[..., :D].reshape(batch, length, HEADS, HEAD_DIM)
    keys = joined[..., D:split_key].reshape(batch, length, KV_HEADS, HEAD_DIM)
    values = joined[..., split_key:].reshape(batch, length, KV_HEADS, HEAD_DIM)
    return (
        rotate(normalize(query, query_gain), angles),
        rotate(normalize(keys, key_gain), angles),
        values,
    )


def allowed_mask(key_start, count, positions, start_of):
    key_place = key_start + jnp.arange(count)
    allowed = (key_place[None, None, :] <= positions[None, :, None]) & (
        key_place[None, None, :] >= start_of[:, :, None]
    )
    return allowed[:, None, None]


def attend_piece(state, query_low, pair, key_start, positions, start_of):
    top, total, summed = state
    batch, count = (pair.shape[1], pair.shape[2])
    keys = pair[0].reshape(batch, count, KV_HEADS, HEAD_DIM)
    values = pair[1].reshape(batch, count, KV_HEADS, HEAD_DIM)
    mask = allowed_mask(key_start, count, positions, start_of)
    scores = jnp.einsum(
        "bqgjd,bkgd->bgjqk", query_low, keys, preferred_element_type=jnp.float32
    ) * HEAD_DIM ** (-0.5)
    scores = jnp.where(mask, scores, NEGATIVE)
    fresh = jnp.maximum(top, jnp.max(scores, axis=-1))
    decay = jnp.exp(top - fresh)
    weights = jnp.where(mask, jnp.exp(scores - fresh[..., None]), 0.0)
    total = decay * total + jnp.sum(weights, axis=-1)
    summed = decay[..., None] * summed + jnp.einsum(
        "bgjqk,bkgd->bgjqd",
        weights.astype(jnp.bfloat16),
        values,
        preferred_element_type=jnp.float32,
    )
    return (fresh, total, summed)


def back_piece(
    query_slope,
    pair_slope,
    query_low,
    slope_low,
    log_total,
    offset,
    pair,
    key_start,
    positions,
    start_of,
):
    batch, count = (pair.shape[1], pair.shape[2])
    keys = pair[0].reshape(batch, count, KV_HEADS, HEAD_DIM)
    values = pair[1].reshape(batch, count, KV_HEADS, HEAD_DIM)
    scale = HEAD_DIM ** (-0.5)
    mask = allowed_mask(key_start, count, positions, start_of)
    scores = (
        jnp.einsum("bqgjd,bkgd->bgjqk", query_low, keys, preferred_element_type=jnp.float32) * scale
    )
    chance = jnp.where(mask, jnp.exp(jnp.where(mask, scores, NEGATIVE) - log_total[..., None]), 0.0)
    slope_chance = jnp.einsum(
        "bqgjd,bkgd->bgjqk", slope_low, values, preferred_element_type=jnp.float32
    )
    slope_scores = jnp.where(mask, chance * (slope_chance - offset[..., None]), 0.0).astype(
        jnp.bfloat16
    )
    query_slope = (
        query_slope
        + jnp.einsum("bgjqk,bkgd->bqgjd", slope_scores, keys, preferred_element_type=jnp.float32)
        * scale
    )
    slope_keys = (
        jnp.einsum("bgjqk,bqgjd->bkgd", slope_scores, query_low, preferred_element_type=jnp.float32)
        * scale
    )
    slope_values = jnp.einsum(
        "bgjqk,bqgjd->bkgd",
        chance.astype(jnp.bfloat16),
        slope_low,
        preferred_element_type=jnp.float32,
    )
    width = KV_HEADS * HEAD_DIM
    pair_slope = pair_slope + jnp.stack(
        [slope_keys.reshape(batch, count, width), slope_values.reshape(batch, count, width)]
    )
    return (query_slope, pair_slope)


def pass_on(pair_slope):
    return shifted(pair_slope.astype(jnp.bfloat16), "seq", 1).astype(pair_slope.dtype)


def on_device(
    layer_input,
    document_lengths,
    attention_gain,
    attention_in,
    query_gain,
    key_gain,
    attention_out,
    feed_gain,
    feed_weight,
    cotangent,
):
    batch, length = (layer_input.shape[0], layer_input.shape[1])
    tokens = batch * length
    groups = HEADS // KV_HEADS
    place = lax.axis_index("seq")
    positions = place * length + jnp.arange(length)
    last = place * length + length - 1
    ends = jnp.cumsum(document_lengths, axis=1)
    start_of = jnp.sum(
        jnp.where(positions[None, :, None] >= ends[:, None, :], document_lengths[:, None, :], 0),
        axis=2,
    )
    half = HEAD_DIM // 2
    frequency = jnp.exp(
        jnp.arange(half).astype(jnp.float32) * (-2.0 * math.log(10000.0) / HEAD_DIM)
    )
    angles = (positions[None, :] - start_of).astype(jnp.float32)[..., None] * frequency
    inputs = layer_input.astype(jnp.float32).reshape(tokens, D)
    normed = normalize(inputs, attention_gain).astype(jnp.bfloat16)
    joined = add_rows(normed, lax.all_gather(attention_in, ("dp", "seq"), axis=0, tiled=True))
    joined = joined.reshape(batch, length, attention_in.shape[1])
    query, keys, values = prepare(joined, query_gain, key_gain, angles)
    query_low = query.astype(jnp.bfloat16).reshape(batch, length, KV_HEADS, groups, HEAD_DIM)
    width = KV_HEADS * HEAD_DIM
    pair = jnp.stack(
        [keys.reshape(batch, length, width), values.reshape(batch, length, width)]
    ).astype(jnp.bfloat16)

    def attend_at(state, piece, key_start):

        def attend_compute(state, piece, key_start):
            return attend_piece(state, query_low, piece, key_start, positions, start_of)

        def attend_keep(state, piece, key_start):
            return state

        return lax.cond(
            (key_start >= 0) & (key_start <= last),
            attend_compute,
            attend_keep,
            state,
            piece,
            key_start,
        )

    state = (
        jnp.full((batch, KV_HEADS, groups, length), NEGATIVE, jnp.float32),
        jnp.zeros((batch, KV_HEADS, groups, length), jnp.float32),
        jnp.zeros((batch, KV_HEADS, groups, length, HEAD_DIM), jnp.float32),
    )
    state = attend_at(state, pair, place * length)

    def cycle_step(step, carry):
        state, moving = carry
        moving = shifted_2(moving, "seq", 1)
        state = attend_at(state, moving, (place - step) * length)
        return (state, moving)

    state, moving = lax.fori_loop(1, lax.axis_size("seq"), cycle_step, (state, pair))
    top, total, summed = state
    log_total = top + jnp.log(total)
    attended = jnp.transpose(summed / total[..., None], (0, 3, 1, 2, 4))
    attended_low = attended.reshape(tokens, D).astype(jnp.bfloat16)
    branch = add_rows(
        attended_low, lax.all_gather(attention_out, ("dp", "seq"), axis=0, tiled=True)
    )
    resid = inputs + branch
    normed_feed = normalize(resid, feed_gain).astype(jnp.bfloat16)
    piece = lax.all_gather(feed_weight, ("dp", "seq"), axis=0, tiled=True)
    gate = against(normed_feed, piece[:, :D])
    upward = against(normed_feed, piece[:, D : 2 * D])
    hidden = (jax.nn.silu(gate) * upward).astype(jnp.bfloat16)
    mixed = jnp.dot(hidden, piece[:, 2 * D :], preferred_element_type=jnp.float32)
    layer_output = (resid + mixed).astype(jnp.bfloat16).reshape(batch, length, D)
    slope_out = cotangent.reshape(tokens, D)

    def feed_back(piece):
        gate = against(normed_feed, piece[:, :D])
        upward = against(normed_feed, piece[:, D : 2 * D])
        hidden = (jax.nn.silu(gate) * upward).astype(jnp.bfloat16)
        slope_hidden = against(slope_out, piece[:, 2 * D :])
        unused, pullback = jax.vjp(lambda first, second: jax.nn.silu(first) * second, gate, upward)
        slope_gate, slope_up = pullback(slope_hidden)
        slope_gate = slope_gate.astype(jnp.bfloat16)
        slope_up = slope_up.astype(jnp.bfloat16)
        total = jnp.dot(slope_gate, piece[:, :D], preferred_element_type=jnp.float32)
        total = total + jnp.dot(slope_up, piece[:, D : 2 * D], preferred_element_type=jnp.float32)
        stash_gate = jnp.stack([slope_gate, slope_up])
        return (total, stash_gate, hidden)

    slope_normed, stash_gate, stash_hidden = feed_back(
        lax.all_gather(feed_weight, ("dp", "seq"), axis=0, tiled=True)
    )
    hidden = stash_hidden
    feed_weight_gradient = lax.psum_scatter(
        jnp.concatenate(
            [
                across(stash_gate[0], normed_feed),
                across(stash_gate[1], normed_feed),
                across(hidden, slope_out),
            ],
            axis=1,
        ),
        ("dp", "seq"),
        scatter_dimension=0,
        tiled=True,
    )
    unused, norm_pull = jax.vjp(normalize, resid, feed_gain)
    slope_resid, feed_gain_part = norm_pull(slope_normed)
    slope_resid = slope_resid + slope_out.astype(jnp.float32)
    slope_branch = slope_resid.astype(jnp.bfloat16)
    slope_attended = against(
        slope_branch, lax.all_gather(attention_out, ("dp", "seq"), axis=0, tiled=True)
    )
    slope_low = slope_attended.astype(jnp.bfloat16).reshape(
        batch, length, KV_HEADS, groups, HEAD_DIM
    )
    offset = jnp.sum(slope_low.astype(jnp.float32) * attended, axis=-1)
    offset = jnp.transpose(offset, (0, 2, 3, 1))

    def back_at(query_slope, pair_slope, piece, key_start):

        def back_compute(query_slope, pair_slope, piece, key_start):
            return back_piece(
                query_slope,
                pair_slope,
                query_low,
                slope_low,
                log_total,
                offset,
                piece,
                key_start,
                positions,
                start_of,
            )

        def back_keep(query_slope, pair_slope, piece, key_start):
            return (query_slope, pair_slope)

        return lax.cond(
            (key_start >= 0) & (key_start <= last),
            back_compute,
            back_keep,
            query_slope,
            pair_slope,
            piece,
            key_start,
        )

    query_slope, pair_slope = back_at(
        jnp.zeros(query_low.shape, jnp.float32),
        jnp.zeros(pair.shape, jnp.float32),
        pair,
        place * length,
    )

    def back_step(step, carry):
        query_slope, pair_slope, moving = carry
        pair_slope = pass_on(pair_slope)
        moving = shifted_2(moving, "seq", 1)
        query_slope, pair_slope = back_at(query_slope, pair_slope, moving, (place - step) * length)
        return (query_slope, pair_slope, moving)

    query_slope, pair_slope, moving = lax.fori_loop(
        1, lax.axis_size("seq"), back_step, (query_slope, pair_slope, pair)
    )
    pair_slope = pass_on(pair_slope)
    unused, prepare_pull = jax.vjp(
        lambda first, second, third: prepare(first, second, third, angles),
        joined,
        query_gain,
        key_gain,
    )
    slope_joined, query_gain_part, key_gain_part = prepare_pull(
        (
            query_slope.reshape(batch, length, HEADS, HEAD_DIM),
            pair_slope[0].reshape(batch, length, KV_HEADS, HEAD_DIM),
            pair_slope[1].reshape(batch, length, KV_HEADS, HEAD_DIM),
        )
    )
    slope_joined = slope_joined.reshape(tokens, attention_in.shape[1]).astype(jnp.bfloat16)
    attention_terms_mine = lax.psum_scatter(
        jnp.concatenate([across(normed, slope_joined), across(attended_low, slope_branch)], axis=1),
        ("dp", "seq"),
        scatter_dimension=0,
        tiled=True,
    )
    attention_in_gradient = attention_terms_mine[:, : attention_in.shape[1]]
    attention_out_gradient = attention_terms_mine[:, attention_in.shape[1] :]
    slope_first = against(
        slope_joined, lax.all_gather(attention_in, ("dp", "seq"), axis=0, tiled=True)
    )
    unused, first_pull = jax.vjp(normalize, inputs, attention_gain)
    slope_inputs, attention_gain_part = first_pull(slope_first)
    input_gradient = (slope_resid + slope_inputs).astype(jnp.bfloat16).reshape(batch, length, D)
    gain_totals = lax.psum(
        (attention_gain_part, query_gain_part, key_gain_part, feed_gain_part), ("dp", "seq")
    )
    return (
        layer_output,
        input_gradient,
        gain_totals[0],
        attention_in_gradient,
        gain_totals[1],
        gain_totals[2],
        attention_out_gradient,
        gain_totals[3],
        feed_weight_gradient,
    )


def solution(mesh):
    placed = (
        P("dp", "seq", None),
        P("dp", None),
        P(),
        P(("dp", "seq"), None),
        P(),
        P(),
        P(("dp", "seq"), None),
        P(),
        P(("dp", "seq"), None),
        P("dp", "seq", None),
    )
    return jax.shard_map(
        on_device,
        mesh=mesh,
        in_specs=placed,
        out_specs=(
            P("dp", "seq", None),
            P("dp", "seq", None),
            P(),
            P(("dp", "seq"), None),
            P(),
            P(),
            P(("dp", "seq"), None),
            P(),
            P(("dp", "seq"), None),
        ),
        check_vma=False,
    )
```

profile of v0, /device:TPU:0, one launch (start us, length us, event | category | flops | bytes accessed | tf_op | source)
XLA Modules:
  0.0 3002.5 jit_solution(6363714915622166425)
XLA Ops:
  10.2 98.6 %all-gather.4.cloned.1.call-done = bf16[2048,3072]{1,0:T(8,128)(2,1)} async-done(((bf16[64,3072]{1,0:T(8,128)(2,1)}), bf16[2048,3072]{1,0:T(8,128)(2,1)}) %all-gather.4.cloned.1.call-update) | async-done | bytes 12582928 | tf_op jit(solution)/shard_map/all_gather | solution.py:188
  121.7 62.7 %while.38 = (s32[]{:T(128)}, f32[1,8,4,128]{3,2,1,0:T(4,128)S(1)}, f32[1,8,4,128]{3,2,1,0:T(4,128)S(1)}, f32[1,8,4,128,64]{3,4,2,1,0:T(8,128)S(1)}, bf16[2,1,128...) while((s32[]{:T(128)}, f32[1,8,4,128]{3,2,1,0:T(4,128)S(1)}, ...), condition=%wide.region_14.15_spmd.clone, body=%wide.region_9.14_spmd.clone.sunk | while | flops 141619456 | bytes 11603807 | solution.py:227
  133.7 9.9 collective-permute-start
  144.8 8.6 collective-permute-start
  163.2 12.3 collective-permute-start
  195.8 513.9 %all-gather.8.cloned.1.call-done = bf16[8192,6144]{1,0:T(8,128)(2,1)} async-done(((bf16[256,6144]{1,0:T(8,128)(2,1)}), bf16[8192,6144]{1,0:T(8,128)(2,1)}) %all-gather.8.cloned.1.call-update) | async-done | bytes 100663312 | tf_op jit(solution)/shard_map/all_gather | solution.py:237
  709.7 17.5 fusion.77
  727.2 17.5 fusion.71
  744.7 20.9 fusion.85
  765.6 14.7 fusion.75
  780.3 15.4 multiply_reduce_fusion
  797.6 8.1 fusion.128
  812.9 75.3 %while.39 = (s32[]{:T(128)}, f32[1,128,8,4,64]{1,4,3,2,0:T(8,128)S(1)}, f32[2,1,128,512]{2,3,1,0:T(8,128)S(1)}, bf16[2,1,128,512]{2,3,1,0:T(8,128)(2,1)}, s32[]{...) while((s32[]{:T(128)}, ...), condition=%wide.region_23.24_spmd.clone, body=%wide.region_20.23_spmd.clone.sunk | while | flops 341426432 | bytes 20926360 | solution.py:332
  902.4 10.4 fusion.118
  912.8 28.3 pad_maximum_fusion.2
  942.2 26.3 fusion.144
  968.5 23.5 fusion.145
  992.0 23.7 fusion.121
  1015.7 135.6 %pad_maximum_fusion.1 = f32[8192,6144]{0,1:T(8,128)} fusion(f32[8192,2048]{0,1:T(8,128)} %fusion.121, f32[8192,2048]{0,1:T(8,128)} %fusion.145, f32[8192,2048]{0,1:T(8,128)} %fusion.144), kind=kLoop, calls=%fused_computation.99 | loop fusion | flops 100663296 | bytes 402653184 | tf_op jit(solution)/shard_map/concatenate | solution.py:264
  1152.5 15.0 fusion.96
  1167.6 10.1 fusion.106
  1177.8 47.1 %all-reduce.7 = (f32[2048]{0:T(1024)}, f32[64]{0:T(128)}, f32[64]{0:T(128)}, f32[2048]{0:T(1024)}) all-reduce(f32[2048]{0:T(1024)S(1)} %get-tuple-element.710, f32[64]{0:T(128)S(1)} %copy-done.54, f32[64]{0:T(128)S(1)} %copy-done.53, f32[2048]{0:T(1024)S(1)} %copy-done.48), channel_id=1, replica_groups=mesh['dp'=4,'seq'=8] {'dp','seq'}, use_global_device_ids=true, to_apply=%region_28.29 | all-reduce | flops 4224 | bytes 33792 | tf_op jit(solution)/shard_map/psum | solution.py:364
  1227.3 160.1 %reduce-scatter.3.cloned.1.call-done = f32[64,5120]{1,0:T(8,128)} async-done(((f32[2048,5120]{1,0:T(8,128)}), f32[64,5120]{1,0:T(8,128)}) %reduce-scatter.3.cloned.1.call-update) | async-done | bytes 1310736 | tf_op jit(solution)/shard_map/reduce_scatter | solution.py:350
  1391.3 1597.8 %reduce-scatter.5.cloned.1.call-done = f32[256,6144]{0,1:T(8,128)} async-done(((f32[8192,6144]{0,1:T(8,128)}), f32[256,6144]{0,1:T(8,128)}) %reduce-scatter.5.cloned.1.call-update) | async-done | bytes 6291472 | tf_op jit(solution)/shard_map/reduce_scatter | solution.py:263
  (304 shorter events, 176.4 us)
Async XLA Ops:
  7.2 101.6 %all-gather.4.cloned.1.call-start = ((), (), s32[]{:S(2)}) async-start(), calls=%async_computation.2 | async-start | bytes 12976128 | tf_op jit(solution)/shard_map/all_gather | solution.py:188
  7.9 182.7 %all-gather.6.cloned.1.call-start = ((), (), s32[]{:S(2)}) async-start(), calls=%async_computation.3 | async-start | bytes 8650752 | tf_op jit(solution)/shard_map/all_gather | solution.py:233
  8.7 701.0 %all-gather.8.cloned.1.call-start = ((), (), s32[]{:S(2)}) async-start(), calls=%async_computation.4 | async-start | bytes 103809024 | tf_op jit(solution)/shard_map/all_gather | solution.py:237
  9.4 1378.0 %reduce-scatter.3.cloned.1.call-start = ((), (), s32[]{:S(2)}) async-start(), calls=%async_computation.5 | async-start | bytes 43253760 | tf_op jit(solution)/shard_map/reduce_scatter | solution.py:350
  125.1 8.6 collective-permute-start
  133.7 11.0 collective-permute-start
  144.8 9.8 collective-permute-start
  154.6 8.6 collective-permute-start
  163.2 13.6 collective-permute-start
  176.8 7.6 collective-permute-start
  812.9 6.7 collective-permute-start.1
  813.2 6.5 collective-permute-start.2
  820.5 8.1 collective-permute-start.1
  830.7 10.1 collective-permute-start.1
  833.7 8.4 collective-permute-start.2
  842.9 7.3 collective-permute-start.1
  845.9 5.6 collective-permute-start.2
  852.3 10.5 collective-permute-start.1
  858.5 5.6 collective-permute-start.2
  864.8 9.7 collective-permute-start.1
  868.8 7.1 collective-permute-start.2
  876.6 9.8 collective-permute-start.1
  890.5 10.3 collective-permute-start.3
  941.2 2048.0 %reduce-scatter.5.cloned.1.call-start = ((), (), s32[]{:S(2)}) async-start(), calls=%async_computation.6 | async-start | bytes 207618048 | tf_op jit(solution)/shard_map/reduce_scatter | solution.py:263
  (63 other events, 2307.2 us)
Sparse Core Ops, SparseCore 0:
  10.9 97.8 all-gather.3
  111.6 78.9 all-gather.5
  193.5 516.0 all-gather.7
  941.3 446.0 reduce-scatter.2
  1393.7 1595.4 reduce-scatter.4
where the time goes:
time: 3010 us; the launch traced here: 3000 us
  waiting for transfers between devices  2400 us (80%)
  matrix products  221 us (7%)
  other arithmetic  175 us (6%)
  starting transfers between devices  117 us (4%)
  blocking collectives  47.1 us (2%)
    reduce_scatter x1, waiting for transfers between devices, on_device(): lax.psum_scatter(jnp.concatenate([across(stash_gate[0], normed_feed), acr...  1600 us
    all_gather x1, waiting for transfers between devices, on_device(): piece = lax.all_gather(feed_weight, ('dp', 'seq'), axis=0, tiled=True)  514 us
    reduce_scatter x1, waiting for transfers between devices, on_device(): lax.psum_scatter(jnp.concatenate([across(normed, slope_joined), across(at...  160 us
    concatenate x1, other arithmetic, on_device(): jnp.concatenate([across(stash_gate[0], normed_feed), across(stash_gate[1]...  136 us
    all_gather x1, waiting for transfers between devices, on_device(): lax.all_gather(attention_in, ('dp', 'seq'), axis=0, tiled=True)  98.6 us
    dot_general x5, matrix products, across(): lax.dot_general(left, right, (((0,), (0,)), ((), ())), preferred_element_...  92 us
    ppermute x14, starting transfers between devices, shifted_2(): lax.ppermute(value, axis, [(source, source + steps) for source in range(i...  87.4 us
    dot_general x5, matrix products, against(): lax.dot_general(left, right, (((1,), (1,)), ((), ())), preferred_element_...  69 us
  transfers between devices with their start and end apart: 27, of which 21 were waited for; matrix products, arithmetic and copies ran while one was open for 9% of the time, Pallas kernels for 0%

commit v1 on v0

v1 whole, which is shorter than its diff:
```python
import functools
import math

import jax
import jax.numpy as jnp
import numpy as np
from jax import lax
from jax.experimental import pallas as pl
from jax.experimental.pallas import tpu as pltpu
from jax.sharding import PartitionSpec as P

D = 2048
HEADS = 32
KV_HEADS = 8
HEAD_DIM = 64
EPSILON = 1e-06
NEGATIVE = -1e30
AXES = ("dp", "seq")
CHUNKS = 2
F32 = jnp.float32
BF16 = jnp.bfloat16


def nt(left, right):
    return lax.dot_general(left, right, (((1,), (1,)), ((), ())), preferred_element_type=F32)


def nn(left, right):
    return jnp.dot(left, right, preferred_element_type=F32)


def tn(left, right):
    return lax.dot_general(left, right, (((0,), (0,)), ((), ())), preferred_element_type=F32)


def normalize(value, gain):
    return value * lax.rsqrt(jnp.mean(value * value, axis=-1, keepdims=True) + EPSILON) * gain


def rotate(value, cosine, sine):
    half = value.shape[-1] // 2
    first = value[..., :half]
    second = value[..., half:]
    return jnp.concatenate(
        [first * cosine - second * sine, second * cosine + first * sine], axis=-1
    )


class Links:
    def __init__(self, dp, seq):
        self.dp, self.seq, self.count = dp, seq, dp * seq
        self.plane = [1 << b for b in range(1, seq.bit_length() - 1)]
        self.depth = [seq << b for b in range(dp.bit_length() - 1)]

    def send(self, value, target):
        return lax.ppermute(value, AXES, [(i, target(i)) for i in range(self.count)])

    def flip(self, value, mask):
        return self.send(value, lambda i: i ^ mask)

    def order(self, index):
        return self.plane if index % 2 == 0 else self.plane[::-1]

    def level(self, value, level):
        return self.send(value, lambda i: i ^ self.order(i)[level])

    def slot_masks(self, index):
        half = self.seq // 2

        def mask(i, slot):
            return functools.reduce(
                lambda a, b: a ^ b,
                [m for level, m in enumerate(self.order(i)) if slot >> level & 1],
                0,
            )

        return [mask(index, s) for s in range(half)] + [1 ^ mask(index ^ 1, s) for s in range(half)]

    def seq_gather(self, value):
        pieces = [value]
        for slot in range(1, self.seq // 2):
            level = slot.bit_length() - 1
            pieces.append(self.level(pieces[slot ^ (1 << level)], level))
        return pieces + [self.flip(piece, 1) for piece in pieces]

    def seq_scatter(self, parts):
        half = self.seq // 2
        terms = [[parts[s], self.flip(parts[s + half], 1)] for s in range(half)]
        for slot in range(half - 1, 0, -1):
            level = slot.bit_length() - 1
            terms[slot ^ (1 << level)].append(self.level(total(terms[slot]).astype(BF16), level))
        return total(terms[0])

    def tree(self, bits):
        groups = {bit: bit if bit in self.plane else 0 for bit in bits}
        load = {group: 0 for group in groups.values()}
        far = [bit for bit in bits if bit in self.depth[1:]]
        parent = {}
        slots = sorted(
            (sum(bit for k, bit in enumerate(bits) if pick >> k & 1) for pick in range(1, 1 << len(bits))),
            key=lambda slot: (bin(slot).count("1"), slot),
        )

        def choices(slot):
            inside = [bit for bit in bits if slot & bit]
            near = [bit for bit in inside if bit not in far]
            return near or [max(inside)]

        for slot in sorted(slots, key=lambda slot: (len({groups[b] for b in choices(slot)}), slot)):
            bit = min(choices(slot), key=lambda b: (load[groups[b]], -b))
            load[groups[bit]] += 1
            parent[slot] = bit
        return [(slot, parent[slot]) for slot in slots]

    def gather(self, value, tree):
        pieces = {0: value}
        for slot, bit in tree:
            pieces[slot] = self.flip(pieces[slot ^ bit], bit)
        return [pieces[slot] for slot in [0] + [s for s, _ in tree]]

    def scatter(self, parts, tree):
        terms = {slot: [part] for slot, part in zip([0] + [s for s, _ in tree], parts)}
        for slot, bit in reversed(tree):
            terms[slot ^ bit].append(self.flip(total(terms[slot]).astype(BF16), bit))
        return total(terms[0])


def total(terms):
    result = terms[0].astype(F32)
    for term in terms[1:]:
        result = result + term.astype(F32)
    return result


def attend_kernel(q_ref, k_ref, v_ref, place_ref, start_ref, key_place_ref, o_ref, lse_ref):
    heads = q_ref.shape[0]
    keys, values = k_ref[...], v_ref[...]
    key_place = key_place_ref[...]
    allowed = (key_place <= place_ref[...]) & (key_place >= start_ref[...])
    for head in range(heads):
        scores = nt(q_ref[head], keys) * HEAD_DIM ** (-0.5)
        scores = jnp.where(allowed, scores, NEGATIVE)
        top = jnp.max(scores, axis=-1, keepdims=True)
        weights = jnp.exp(scores - top)
        whole = jnp.sum(weights, axis=-1, keepdims=True)
        out = nn(weights.astype(BF16), values) / whole
        o_ref[:, head * HEAD_DIM : (head + 1) * HEAD_DIM] = out.astype(BF16)
        lse_ref[:, head : head + 1] = top + jnp.log(whole)


def attend_back_kernel(
    q_ref, k_ref, v_ref, do_ref, lse_ref, place_ref, start_ref, key_place_ref, dq_ref, dk_ref, dv_ref
):
    heads = q_ref.shape[0]
    scale = HEAD_DIM ** (-0.5)

    @pl.when(pl.program_id(0) == 0)
    def _():
        dk_ref[...] = jnp.zeros_like(dk_ref)
        dv_ref[...] = jnp.zeros_like(dv_ref)

    keys, values = k_ref[...], v_ref[...]
    key_place = key_place_ref[...]
    allowed = (key_place <= place_ref[...]) & (key_place >= start_ref[...])
    for head in range(heads):
        query = q_ref[head]
        slope = do_ref[:, head * HEAD_DIM : (head + 1) * HEAD_DIM]
        scores = jnp.where(allowed, nt(query, keys) * scale, NEGATIVE)
        chance = jnp.exp(scores - lse_ref[:, head : head + 1])
        slope_chance = nt(slope, values)
        moved = chance * slope_chance
        offset = jnp.sum(moved, axis=-1, keepdims=True)
        slope_scores = (moved - chance * offset).astype(BF16)
        dq_ref[head] = nn(slope_scores, keys) * scale
        dk_ref[...] += tn(slope_scores, query) * scale
        dv_ref[...] += tn(chance.astype(BF16), slope)


def attend(query, keys, values, place, start, block):
    heads, length, width = query.shape
    rows = pl.BlockSpec((block, 1), lambda i: (i, 0))
    whole = pl.BlockSpec((length, width), lambda i: (0, 0))
    return pl.pallas_call(
        attend_kernel,
        grid=(length // block,),
        in_specs=[
            pl.BlockSpec((heads, block, width), lambda i: (0, i, 0)),
            whole,
            whole,
            rows,
            rows,
            pl.BlockSpec((1, length), lambda i: (0, 0)),
        ],
        out_specs=[
            pl.BlockSpec((block, heads * width), lambda i: (i, 0)),
            pl.BlockSpec((block, heads), lambda i: (i, 0)),
        ],
        out_shape=[
            jax.ShapeDtypeStruct((length, heads * width), BF16),
            jax.ShapeDtypeStruct((length, heads), F32),
        ],
        cost_estimate=pl.CostEstimate(
            flops=4 * heads * length * length * 256,
            transcendentals=heads * length * length,
            bytes_accessed=8 * heads * length * width,
        ),
        name="attend",
    )(query, keys, values, place[:, None], start[:, None], place[None, :])


def attend_back(query, keys, values, slope, lse, place, start, block):
    heads, length, width = query.shape
    rows = pl.BlockSpec((block, 1), lambda i: (i, 0))
    whole = pl.BlockSpec((length, width), lambda i: (0, 0))
    byhead = pl.BlockSpec((heads, block, width), lambda i: (0, i, 0))
    return pl.pallas_call(
        attend_back_kernel,
        grid=(length // block,),
        in_specs=[
            byhead,
            whole,
            whole,
            pl.BlockSpec((block, heads * width), lambda i: (i, 0)),
            pl.BlockSpec((block, heads), lambda i: (i, 0)),
            rows,
            rows,
            pl.BlockSpec((1, length), lambda i: (0, 0)),
        ],
        out_specs=[byhead, whole, whole],
        out_shape=[
            jax.ShapeDtypeStruct((heads, length, width), F32),
            jax.ShapeDtypeStruct((length, width), F32),
            jax.ShapeDtypeStruct((length, width), F32),
        ],
        cost_estimate=pl.CostEstimate(
            flops=10 * heads * length * length * 256,
            transcendentals=heads * length * length,
            bytes_accessed=16 * heads * length * width,
        ),
        name="attend_back",
    )(query, keys, values, slope, lse, place[:, None], start[:, None], place[None, :])


def split(value, count):
    size = value.shape[0] // count
    return [value[i * size : (i + 1) * size] for i in range(count)]


def feed(normed, slope, gate_up, down):
    both = nt(normed, gate_up)
    hidden_count = down.shape[0]
    gate, up = both[:, :hidden_count], both[:, hidden_count:]
    slope_hidden = nt(slope, down)
    bend = jax.nn.sigmoid(gate)
    curve = gate * bend
    hidden = (curve * up).astype(BF16)
    slope_gate = (slope_hidden * up * (bend * (1.0 + gate * (1.0 - bend)))).astype(BF16)
    slope_up = (slope_hidden * curve).astype(BF16)
    slope_both = jnp.concatenate([slope_gate, slope_up], axis=1)
    return hidden, slope_both


def on_device(
    layer_input,
    document_lengths,
    attention_gain,
    attention_in,
    query_gain,
    key_gain,
    attention_out,
    feed_gain,
    feed_weight,
    cotangent,
):
    dp, seq = lax.axis_size("dp"), lax.axis_size("seq")
    links = Links(dp, seq)
    count = links.count
    batch, length = layer_input.shape[0], layer_input.shape[1]
    tokens = batch * length
    here_dp, here = lax.axis_index("dp"), lax.axis_index("seq")
    q_heads = HEADS // seq
    shared = seq // KV_HEADS
    width = KV_HEADS * HEAD_DIM
    rows = attention_in.shape[0]

    masks = jnp.asarray(np.array([links.slot_masks(0), links.slot_masks(1)], np.int32))
    slot_seq = here ^ jnp.where(here % 2 == 0, masks[0], masks[1])
    place = (slot_seq[:, None] * length + jnp.arange(length)[None, :]).reshape(-1)
    lengths = document_lengths[0]
    ends = jnp.cumsum(lengths)
    start = jnp.sum(jnp.where(place[:, None] >= ends[None, :], lengths[None, :], 0), axis=1)
    half = HEAD_DIM // 2
    frequency = jnp.exp(jnp.arange(half).astype(F32) * (-2.0 * math.log(10000.0) / HEAD_DIM))
    angles = (place - start).astype(F32)[:, None] * frequency
    cosine, sine = jnp.cos(angles), jnp.sin(angles)

    w_query = attention_in[:, :D].reshape(rows, seq, q_heads * HEAD_DIM)
    w_key = attention_in[:, D : D + width].reshape(rows, KV_HEADS, HEAD_DIM)
    w_value = attention_in[:, D + width :].reshape(rows, KV_HEADS, HEAD_DIM)
    w_mine = jnp.concatenate(
        [w_query, jnp.repeat(w_key, shared, axis=1), jnp.repeat(w_value, shared, axis=1)], axis=2
    )
    w_mine = jnp.transpose(w_mine, (1, 0, 2))
    columns = w_mine.shape[2]
    w_in = lax.all_to_all(
        jnp.broadcast_to(w_mine[None], (dp,) + w_mine.shape).reshape(count, rows, columns),
        AXES, 0, 0, tiled=True,
    ).reshape(D, columns)

    w_slots = [
        links.send(attention_out, lambda i, m=m: ((i % dp + m) % dp) * seq + i // dp)
        for m in range(dp)
    ]
    w_out = jnp.concatenate(w_slots[::-1] + w_slots[::-1], axis=0)
    out_rows = dp * rows
    w_out = lax.dynamic_slice_in_dim(w_out, ((dp - 1 - here_dp) % dp) * rows, out_rows, 0)

    inputs = layer_input.astype(F32).reshape(tokens, D)
    normed = normalize(inputs, attention_gain).astype(BF16)
    normed_all = jnp.concatenate(links.seq_gather(normed), axis=0)
    joined = nn(normed_all, w_in)
    whole = normed_all.shape[0]

    def prepare(joined, query_gain, key_gain):
        split_key = q_heads * HEAD_DIM
        query = joined[:, :split_key].reshape(whole, q_heads, HEAD_DIM)
        keys = joined[:, split_key : split_key + HEAD_DIM]
        values = joined[:, split_key + HEAD_DIM :]
        query = rotate(normalize(query, query_gain), cosine[:, None], sine[:, None])
        keys = rotate(normalize(keys, key_gain), cosine, sine)
        return jnp.transpose(query, (1, 0, 2)), keys, values

    query, keys, values = prepare(joined, query_gain, key_gain)
    query, keys, values = query.astype(BF16), keys.astype(BF16), values.astype(BF16)
    attended, lse = attend(query, keys, values, place, start, length)
    branch = links.seq_scatter(split(nn(attended, w_out).astype(BF16), seq))
    resid = inputs + branch
    normed_feed = normalize(resid, feed_gain).astype(BF16)

    tree = links.tree(links.plane + links.depth)
    other = links.flip(feed_weight, 1)
    gate_up = jnp.concatenate(
        [feed_weight[:, :D], other[:, :D], feed_weight[:, D : 2 * D], other[:, D : 2 * D]], axis=0
    )
    down = jnp.concatenate([feed_weight[:, 2 * D :], other[:, 2 * D :]], axis=0)
    slope_out = cotangent.reshape(tokens, D)
    slots = len(tree) + 1
    chunked = []
    for low, slope in zip(split(normed_feed, CHUNKS), split(slope_out, CHUNKS)):
        low_all = jnp.concatenate(links.gather(low, tree), axis=0)
        slope_all = jnp.concatenate(links.gather(slope, tree), axis=0)
        hidden, slope_both = feed(low_all, slope_all, gate_up, down)
        chunked.append((low_all, slope_all, hidden, slope_both))
    slope_normed = jnp.concatenate(
        [
            links.scatter(split(nn(slope_both, gate_up).astype(BF16), slots), tree)
            for _, _, _, slope_both in chunked
        ],
        axis=0,
    )
    unused, norm_pull = jax.vjp(normalize, resid, feed_gain)
    slope_resid, feed_gain_part = norm_pull(slope_normed)
    slope_resid = slope_resid + slope_out.astype(F32)
    slope_branch = slope_resid.astype(BF16)

    mixed = jnp.concatenate(
        [
            links.scatter(split(nn(hidden, down).astype(BF16), slots), tree)
            for _, _, hidden, _ in chunked
        ],
        axis=0,
    )
    layer_output = (resid + mixed).astype(BF16).reshape(batch, length, D)

    low_all, slope_all, hidden, slope_both = [
        jnp.concatenate([chunk[k] for chunk in chunked], axis=0) for k in range(4)
    ]
    grad_both = tn(slope_both, low_all)
    grad_down = tn(hidden, slope_all)
    units = feed_weight.shape[0]
    mine = jnp.concatenate(
        [grad_both[:units], grad_both[2 * units : 3 * units], grad_down[:units]], axis=1
    )
    theirs = jnp.concatenate(
        [grad_both[units : 2 * units], grad_both[3 * units :], grad_down[units:]], axis=1
    )
    feed_weight_gradient = mine + links.flip(theirs.astype(BF16), 1).astype(F32)

    slope_branch_all = jnp.concatenate(links.seq_gather(slope_branch), axis=0)
    slope_low = nt(slope_branch_all, w_out).astype(BF16)
    grad_out = tn(attended, slope_branch_all).astype(BF16)
    grad_out = jnp.concatenate([grad_out, grad_out], axis=0)
    grad_out = lax.dynamic_slice_in_dim(grad_out, ((here_dp + 1) % dp) * rows, out_rows, 0)
    blocks = split(grad_out, dp)[::-1]
    pieces = []
    for m in range(dp):
        pairs = {((i % dp + m) % dp) * seq + i // dp: i for i in range(count)}
        pieces.append(links.send(blocks[m], lambda i, pairs=pairs: pairs[i]))
    attention_out_gradient = total(pieces)

    dq, dk, dv = attend_back(query, keys, values, slope_low, lse, place, start, length)
    unused, prepare_pull = jax.vjp(prepare, joined, query_gain, key_gain)
    slope_joined, query_gain_part, key_gain_part = prepare_pull((dq, dk, dv))
    slope_joined = slope_joined.astype(BF16)
    slope_first = links.seq_scatter(split(nt(slope_joined, w_in).astype(BF16), seq))
    grad_in = tn(normed_all, slope_joined).astype(BF16).reshape(count, rows, columns)
    grad_in = lax.all_to_all(grad_in, AXES, 0, 0, tiled=True).astype(F32)
    grad_in = jnp.sum(grad_in.reshape(dp, seq, rows, columns), axis=0)
    split_key = q_heads * HEAD_DIM
    grad_query = jnp.transpose(grad_in[:, :, :split_key], (1, 0, 2)).reshape(rows, D)
    grad_key = jnp.sum(
        grad_in[:, :, split_key : split_key + HEAD_DIM].reshape(KV_HEADS, shared, rows, HEAD_DIM), axis=1
    )
    grad_value = jnp.sum(
        grad_in[:, :, split_key + HEAD_DIM :].reshape(KV_HEADS, shared, rows, HEAD_DIM), axis=1
    )
    attention_in_gradient = jnp.concatenate(
        [
            grad_query,
            jnp.transpose(grad_key, (1, 0, 2)).reshape(rows, width),
            jnp.transpose(grad_value, (1, 0, 2)).reshape(rows, width),
        ],
        axis=1,
    )
    unused, first_pull = jax.vjp(normalize, inputs, attention_gain)
    slope_inputs, attention_gain_part = first_pull(slope_first)
    input_gradient = (slope_resid + slope_inputs).astype(BF16).reshape(batch, length, D)
    gains = lax.psum(
        jnp.concatenate([attention_gain_part, query_gain_part, key_gain_part, feed_gain_part]), AXES
    )
    cut = [D, D + HEAD_DIM, D + 2 * HEAD_DIM]
    return (
        layer_output,
        input_gradient,
        gains[: cut[0]],
        attention_in_gradient,
        gains[cut[0] : cut[1]],
        gains[cut[1] : cut[2]],
        attention_out_gradient,
        gains[cut[2] :],
        feed_weight_gradient,
    )


def solution(mesh):
    tokens = P("dp", "seq", None)
    rows = P(("dp", "seq"), None)
    return jax.shard_map(
        on_device,
        mesh=mesh,
        in_specs=(tokens, P("dp", None), P(), rows, P(), P(), rows, P(), rows, tokens),
        out_specs=(tokens, tokens, P(), rows, P(), P(), rows, P(), rows),
        check_vma=False,
    )
```

time: 3010 us -> 818 us (0.27)
  waiting for transfers between devices: 2400 us -> 251 us
  matrix products: 221 us -> 79.1 us
  other arithmetic: 175 us -> 56.5 us
  starting transfers between devices: 117 us -> 234 us
  local copies, waits for them, and re-layouts: 23.6 us -> 94.9 us
  Pallas kernels: 0 us -> 39.1 us
    reduce_scatter x2 -> x0, waiting for transfers between devices: 1760 us -> none  [the longest x1 1600 us: on_device(): lax.psum_scatter(jnp.concatenate([across(stash_gate[0], normed_feed), acr...]
    all_gather x3 -> x0, waiting for transfers between devices: 618 us -> none  [the longest x1 514 us: on_device(): piece = lax.all_gather(feed_weight, ('dp', 'seq'), axis=0, tiled=True)]
    ppermute x22 -> x158, waiting for transfers between devices: 24.7 us -> 251 us  [send(): lax.ppermute(value, AXES, [(i, target(i)) for i in range(self.count)])]
    concatenate x2 -> x3, other arithmetic: 164 us -> 3.62 us  [the longest x1 1.76 us: on_device(): jnp.concatenate([grad_both[units:2 * units], grad_both[3 * units:], grad_...]
    dot_general x22 -> x16, matrix products: 221 us -> 79.1 us  [the longest x4 29.9 us: tn(): lax.dot_general(left, right, (((0,), (0,)), ((), ())), preferred_element_...]
    ppermute x22 -> x158, starting transfers between devices: 117 us -> 223 us  [send(): lax.ppermute(value, AXES, [(i, target(i)) for i in range(self.count)])]
    unnamed x122 -> x259, local copies, waits for them, and re-layouts: 12.3 us -> 69.1 us
    pallas_call x0 -> x2, Pallas kernels: none -> 39.1 us  [the longest x1 23.3 us: attend_back(): pl.pallas_call(attend_back_kernel, grid=(length // block,), in_specs=[byh...]
  transfers between devices with their start and end apart: 27 -> 160, of which waited for: 21 -> 60; matrix products, arithmetic and copies ran while one was open for 9% -> 26% of each run, Pallas kernels for 0% -> 5%
where the time goes in v1:
time: 818 us; the launch traced here: 815 us
  waiting for transfers between devices  251 us (31%)
  starting transfers between devices  234 us (29%)
  local copies, waits for them, and re-layouts  94.9 us (12%)
  matrix products  79.1 us (10%)
  blocking collectives  57.8 us (7%)
  other arithmetic  56.5 us (7%)
  Pallas kernels  39.1 us (5%)
    ppermute x158, waiting for transfers between devices, send(): lax.ppermute(value, AXES, [(i, target(i)) for i in range(self.count)])  251 us
    ppermute x158, starting transfers between devices, send(): lax.ppermute(value, AXES, [(i, target(i)) for i in range(self.count)])  223 us
    unnamed x259, local copies, waits for them, and re-layouts  69.1 us
    psum x1, blocking collectives, on_device(): lax.psum(jnp.concatenate([attention_gain_part, query_gain_part, key_gain_...  57.8 us
    dot_general x4, matrix products, tn(): lax.dot_general(left, right, (((0,), (0,)), ((), ())), preferred_element_...  29.9 us
    dot_general x6, matrix products, nt(): lax.dot_general(left, right, (((1,), (1,)), ((), ())), preferred_element_...  26.3 us
    pallas_call x1, Pallas kernels, attend_back(): pl.pallas_call(attend_back_kernel, grid=(length // block,), in_specs=[byh...  23.3 us
    dot_general x6, matrix products, nn(): return jnp.dot(left, right, preferred_element_type=F32)  22.9 us
  transfers between devices with their start and end apart: 160, of which 60 were waited for; matrix products, arithmetic and copies ran while one was open for 26% of the time, Pallas kernels for 5%

profile of v1, /device:TPU:0, one launch (start us, length us, event | category | flops | bytes accessed | tf_op | source)
XLA Modules:
  0.0 815.0 jit_solution(12688343726623629650)
XLA Ops:
  32.5 8.2 %collective-permute-start.9 = (bf16[64,2048]{1,0:T(8,128)(2,1)}, bf16[64,2048]{1,0:T(8,128)(2,1)S(1)}, u32[]{:S(2)}, u32[]{:S(2)}) collective-permute-start(bf16[64,2048]{1,0:T(8,128)(2,1)} %param.17), channel_id=1, source_target_pairs={{0,8},{1,16},{2,24},{3,0},{4,9},{5,17},{6,25},{7,1},{8,10},{9,18},... | collective-permute-start | bytes 786440 | tf_op jit(solution)/shard_map/ppermute | solution.py:56
  42.5 13.1 %collective-permute-done.9 = bf16[64,2048]{1,0:T(8,128)(2,1)S(1)} collective-permute-done((bf16[64,2048]{1,0:T(8,128)(2,1)}, bf16[64,2048]{1,0:T(8,128)(2,1)S(1)}, u32[]{:S(2)}, u32[]{:S(2)}) %collective-permute-start.9) | collective-permute-done | bytes 262176 | tf_op jit(solution)/shard_map/ppermute | solution.py:56
  57.8 22.3 %collective-permute-start.80 = (bf16[64,2048]{1,0:T(8,128)(2,1)S(1)}, bf16[64,2048]{1,0:T(8,128)(2,1)S(1)}, u32[]{:S(2)}, u32[]{:S(2)}) collective-permute-start(bf16[64,2048]{1,0:T(8,128)(2,1)S(1)} %get-tuple-element.138), channel_id=1, source_target_pairs={{0,4},{1,5},{2,6},{3,7},{4,0},{5,1},{6,2},{7,3},{8,12},{9,13},{10,... | collective-permute-start | bytes 786440 | tf_op jit(solution)/shard_map/ppermute | solution.py:56
  93.1 7.0 collective-permute-done.82
  113.6 6.7 collective-permute-done.86
  150.6 6.3 collective-permute-done.2
  209.7 15.8 %attend.1 = (bf16[1024,256]{1,0:T(8,128)(2,1)}, f32[1024,4]{1,0:T(8,128)}) custom-call(bf16[4,1024,64]{2,1,0:T(8,128)(2,1)} %maximum_bitcast_fusion.q_ref, bf16[1024,64]{1,0:T(8,128)(2,1)} %pad_maximum_fusion.5.k_ref, bf16[1024,64]{1,0:T(8,128)(2,1)} %copy.121.v_ref, s32[1024,1]{1,0:T(8,128)} %copy.103.place_ref, s32[1024,1]{1,0:T(8,128)} %copy.104.start_ref, ...), custom_call_target="tpu_custom_call" | custom-call | flops 4294967296 | bytes 2097152 | tf_op jit(solution)/shard_map/attend/pallas_call | solution.py:183
  250.5 9.4 %collective-permute-done.17 = bf16[128,2048]{1,0:T(8,128)(2,1)S(1)} collective-permute-done((bf16[128,2048]{1,0:T(8,128)(2,1)S(1)}, bf16[128,2048]{1,0:T(8,128)(2,1)S(1)}, u32[]{:S(2)}, u32[]{:S(2)}) %collective-permute-start.17) | collective-permute-done | bytes 524320 | tf_op jit(solution)/shard_map/ppermute | solution.py:56
  264.4 14.8 %collective-permute-done.21 = bf16[64,2048]{1,0:T(8,128)(2,1)S(1)} collective-permute-done((bf16[64,2048]{1,0:T(8,128)(2,1)S(1)}, bf16[64,2048]{1,0:T(8,128)(2,1)S(1)}, u32[]{:S(2)}, u32[]{:S(2)}) %collective-permute-start.21) | collective-permute-done | bytes 262176 | tf_op jit(solution)/shard_map/ppermute | solution.py:56
  286.2 7.7 collective-permute-done.22
  357.2 7.0 collective-permute-done.51
  366.8 8.7 %collective-permute-done.37 = bf16[64,2048]{1,0:T(8,128)(2,1)S(1)} collective-permute-done((bf16[64,2048]{1,0:T(8,128)(2,1)S(1)}, bf16[64,2048]{1,0:T(8,128)(2,1)S(1)}, u32[]{:S(2)}, u32[]{:S(2)}) %collective-permute-start.37) | collective-permute-done | bytes 262176 | tf_op jit(solution)/shard_map/ppermute | solution.py:56
  443.4 6.9 fusion.65
  455.1 7.1 fusion.14
  471.0 15.7 %fusion.83 = (bf16[1024,2048]{1,0:T(8,128)(2,1)}, f32[1024,2048]{1,0:T(8,128)}) fusion(bf16[2048,2048]{1,0:T(8,128)(2,1)} %get-tuple-element.142, bf16[1024,512]{1,0:T(8,128)(2,1)} %get-tuple-element.39, bf16[1024,512]{1,0:T(8,128)(2,1)} %get-tuple-element.38, bf16[1024,512]{1,0:T(8,128)(2,1)} %copy-done.70, bf16[1024,512]{1,0:T(8,128)(2,1)} %copy-done.69), kind=kOutput, calls=%fused_computation.360 | convolution fusion | flops 8608808960 | bytes 25165824 | tf_op jit(solution)/shard_map/dot_general | solution.py:33
  534.3 8.7 %collective-permute-done.67 = bf16[64,2048]{1,0:T(8,128)(2,1)S(1)} collective-permute-done((bf16[64,2048]{1,0:T(8,128)(2,1)S(1)}, bf16[64,2048]{1,0:T(8,128)(2,1)S(1)}, u32[]{:S(2)}, u32[]{:S(2)}) %collective-permute-start.67) | collective-permute-done | bytes 262176 | tf_op jit(solution)/shard_map/ppermute | solution.py:56
  563.8 6.6 collective-permute-start.71
  596.4 9.3 %collective-permute-done.139 = bf16[128,2048]{1,0:T(8,128)(2,1)S(1)} collective-permute-done((bf16[128,2048]{1,0:T(8,128)(2,1)S(1)}, bf16[128,2048]{1,0:T(8,128)(2,1)S(1)}, u32[]{:S(2)}, u32[]{:S(2)}) %collective-permute-start.139) | collective-permute-done | bytes 524320 | tf_op jit(solution)/shard_map/ppermute | solution.py:56
  619.1 23.3 %attend_back.1 = (f32[4,1024,64]{2,1,0:T(8,128)}, f32[1024,64]{1,0:T(8,128)}, f32[1024,64]{1,0:T(8,128)}) custom-call(bf16[4,1024,64]{2,1,0:T(8,128)(2,1)} %maximum_bitcast_fusion.q_ref, bf16[1024,64]{1,0:T(8,128)(2,1)} %pad_maximum_fusion.5.k_ref, bf16[1024,64]{1,0:T(8,128)(2,1)} %copy.121.v_ref, bf16[1024,256]{1,0:T(8,128)(2,1)} %convolution_convert_fusion.8.do_ref, ...), custom_call_target="tpu_custom_call" | custom-call | flops 10737418240 | bytes 4194304 | tf_op jit(solution)/shard_map/attend_back/pallas_call | solution.py:216
  682.6 6.4 all-to-all-start.1
  690.8 18.1 %collective-permute-start.156 = (bf16[64,2048]{1,0:T(8,128)(2,1)}, bf16[64,2048]{1,0:T(8,128)(2,1)S(1)}, u32[]{:S(2)}, u32[]{:S(2)}) collective-permute-start(bf16[64,2048]{1,0:T(8,128)(2,1)} %get-tuple-element.121), channel_id=1, source_target_pairs={{0,1},{1,5},{2,9},{3,13},{4,17},{5,21},{6,25},{7,29},{8,2},{9,6},{... | collective-permute-start | bytes 786440 | tf_op jit(solution)/shard_map/ppermute | solution.py:56
  710.7 11.1 %collective-permute-start.148 = (bf16[128,2048]{1,0:T(8,128)(2,1)}, bf16[128,2048]{1,0:T(8,128)(2,1)S(1)}, u32[]{:S(2)}, u32[]{:S(2)}) collective-permute-start(bf16[128,2048]{1,0:T(8,128)(2,1)} %get-tuple-element.46), channel_id=1, source_target_pairs={{0,4},{1,3},{2,6},{3,1},{4,0},{5,7},{6,2},{7,5},{8,12},{9,11},{10,... | collective-permute-start | bytes 1572872 | tf_op jit(solution)/shard_map/ppermute | solution.py:56
  727.0 17.9 %collective-permute-done.155 = bf16[64,2048]{1,0:T(8,128)(2,1)S(1)} collective-permute-done((bf16[64,2048]{1,0:T(8,128)(2,1)}, bf16[64,2048]{1,0:T(8,128)(2,1)S(1)}, u32[]{:S(2)}, u32[]{:S(2)}) %collective-permute-start.155) | collective-permute-done | bytes 262176 | tf_op jit(solution)/shard_map/ppermute | solution.py:56
  749.6 57.8 %psum.7 = f32[4224]{0:T(1024)S(1)} all-reduce(f32[4224]{0:T(1024)S(1)} %concatenate.96), channel_id=1, replica_groups=mesh['dp'=4,'seq'=8] {'dp','seq'}, use_global_device_ids=true, to_apply=%region_14.15 | all-reduce | flops 4224 | bytes 33792 | tf_op jit(solution)/shard_map/psum | solution.py:428
  (687 shorter events, 496.2 us)
Async XLA Ops:
  4.7 106.4 %collective-permute-start = (bf16[128,2048]{1,0:T(8,128)(2,1)}, bf16[128,2048]{1,0:T(8,128)(2,1)}, u32[]{:S(2)}, u32[]{:S(2)}) collective-permute-start(bf16[128,2048]{1,0:T(8,128)(2,1)} %get-tuple-element.33), channel_id=1, source_target_pairs={{0,2},{1,5},{2,0},{3,7},{4,6},{5,1},{6,4},{7,3},{8,10},{9,13},{10,... | collective-permute-start | bytes 1572872 | tf_op jit(solution)/shard_map/ppermute | solution.py:56
  7.6 113.4 %collective-permute-start.1 = (bf16[128,2048]{1,0:T(8,128)(2,1)}, bf16[128,2048]{1,0:T(8,128)(2,1)S(1)}, u32[]{:S(2)}, u32[]{:S(2)}) collective-permute-start(bf16[128,2048]{1,0:T(8,128)(2,1)} %get-tuple-element.33), channel_id=1, source_target_pairs={{0,4},{1,3},{2,6},{3,1},{4,0},{5,7},{6,2},{7,5},{8,12},{9,11},{10,... | collective-permute-start | bytes 1572872 | tf_op jit(solution)/shard_map/ppermute | solution.py:56
  9.2 148.6 %collective-permute-start.3 = (bf16[128,2048]{1,0:T(8,128)(2,1)}, bf16[128,2048]{1,0:T(8,128)(2,1)}, u32[]{:S(2)}, u32[]{:S(2)}) collective-permute-start(bf16[128,2048]{1,0:T(8,128)(2,1)} %get-tuple-element.33), channel_id=1, source_target_pairs={{0,1},{1,0},{2,3},{3,2},{4,5},{5,4},{6,7},{7,6},{8,9},{9,8},{10,11... | collective-permute-start | bytes 1572872 | tf_op jit(solution)/shard_map/ppermute | solution.py:56
  19.1 172.9 %all-to-all-start = ((bf16[32,64,384]{2,1,0:T(8,128)(2,1)}), bf16[32,64,384]{2,1,0:T(8,128)(2,1)S(1)}, u32[]{:S(2)}, u32[]{:S(2)}) async-start(bf16[32,64,384]{2,1,0:T(8,128)(2,1)} %bitcast.3), calls=%async_computation | async-start | bytes 3145728 | tf_op jit(solution)/shard_map/all_to_all | solution.py:305
  107.6 56.5 %collective-permute-start.109 = (bf16[64,2048]{1,0:T(8,128)(2,1)}, bf16[64,2048]{1,0:T(8,128)(2,1)S(1)}, u32[]{:S(2)}, u32[]{:S(2)}) collective-permute-start(bf16[64,2048]{1,0:T(8,128)(2,1)} %get-tuple-element.139), channel_id=1, source_target_pairs={{0,2},{1,3},{2,0},{3,1},{4,6},{5,7},{6,4},{7,5},{8,10},{9,11},{10,... | collective-permute-start | bytes 786440 | tf_op jit(solution)/shard_map/ppermute | solution.py:56
  178.3 50.6 %collective-permute-start.119 = (bf16[64,2048]{1,0:T(8,128)(2,1)}, bf16[64,2048]{1,0:T(8,128)(2,1)}, u32[]{:S(2)}, u32[]{:S(2)}) collective-permute-start(bf16[64,2048]{1,0:T(8,128)(2,1)} %collective-permute-done.114), channel_id=1, source_target_pairs={{0,4},{1,5},{2,6},{3,7},{4,0},{5,1},{6,2},{7,3},{8,12},{9,13},{10,... | collective-permute-start | bytes 786440 | tf_op jit(solution)/shard_map/ppermute | solution.py:56
  179.1 52.2 %collective-permute-start.120 = (bf16[64,2048]{1,0:T(8,128)(2,1)}, bf16[64,2048]{1,0:T(8,128)(2,1)}, u32[]{:S(2)}, u32[]{:S(2)}) collective-permute-start(bf16[64,2048]{1,0:T(8,128)(2,1)} %collective-permute-done.116), channel_id=1, source_target_pairs={{0,4},{1,5},{2,6},{3,7},{4,0},{5,1},{6,2},{7,3},{8,12},{9,13},{10,... | collective-permute-start | bytes 786440 | tf_op jit(solution)/shard_map/ppermute | solution.py:56
  180.4 52.4 %collective-permute-start.122 = (bf16[64,2048]{1,0:T(8,128)(2,1)}, bf16[64,2048]{1,0:T(8,128)(2,1)}, u32[]{:S(2)}, u32[]{:S(2)}) collective-permute-start(bf16[64,2048]{1,0:T(8,128)(2,1)} %collective-permute-done.117), channel_id=1, source_target_pairs={{0,8},{1,9},{2,10},{3,11},{4,12},{5,13},{6,14},{7,15},{8,0},{9,1},... | collective-permute-start | bytes 786440 | tf_op jit(solution)/shard_map/ppermute | solution.py:56
  315.9 37.7 %collective-permute-start.49 = (bf16[64,2048]{1,0:T(8,128)(2,1)S(1)}, bf16[64,2048]{1,0:T(8,128)(2,1)S(1)}, u32[]{:S(2)}, u32[]{:S(2)}) collective-permute-start(bf16[64,2048]{1,0:T(8,128)(2,1)S(1)} %get-tuple-element.132), channel_id=1, source_target_pairs={{0,2},{1,3},{2,0},{3,1},{4,6},{5,7},{6,4},{7,5},{8,10},{9,11},{10,... | collective-permute-start | bytes 786440 | tf_op jit(solution)/shard_map/ppermute | solution.py:56
  317.0 37.5 %collective-permute-start.50 = (bf16[64,2048]{1,0:T(8,128)(2,1)S(1)}, bf16[64,2048]{1,0:T(8,128)(2,1)S(1)}, u32[]{:S(2)}, u32[]{:S(2)}) collective-permute-start(bf16[64,2048]{1,0:T(8,128)(2,1)S(1)} %get-tuple-element.132), channel_id=1, source_target_pairs={{0,4},{1,5},{2,6},{3,7},{4,0},{5,1},{6,2},{7,3},{8,12},{9,13},{10,... | collective-permute-start | bytes 786440 | tf_op jit(solution)/shard_map/ppermute | solution.py:56
  352.4 36.2 %collective-permute-start.42 = (bf16[64,2048]{1,0:T(8,128)(2,1)S(1)}, bf16[64,2048]{1,0:T(8,128)(2,1)S(1)}, u32[]{:S(2)}, u32[]{:S(2)}) collective-permute-start(bf16[64,2048]{1,0:T(8,128)(2,1)S(1)} %get-tuple-element.86), channel_id=1, source_target_pairs={{0,4},{1,5},{2,6},{3,7},{4,0},{5,1},{6,2},{7,3},{8,12},{9,13},{10,... | collective-permute-start | bytes 786440 | tf_op jit(solution)/shard_map/ppermute | solution.py:56
  353.7 35.9 %collective-permute-start.45 = (bf16[64,2048]{1,0:T(8,128)(2,1)S(1)}, bf16[64,2048]{1,0:T(8,128)(2,1)S(1)}, u32[]{:S(2)}, u32[]{:S(2)}) collective-permute-start(bf16[64,2048]{1,0:T(8,128)(2,1)S(1)} %get-tuple-element.85), channel_id=1, source_target_pairs={{0,8},{1,9},{2,10},{3,11},{4,12},{5,13},{6,14},{7,15},{8,0},{9,1},... | collective-permute-start | bytes 786440 | tf_op jit(solution)/shard_map/ppermute | solution.py:56
  421.3 67.7 %collective-permute-start.43 = (bf16[64,2048]{1,0:T(8,128)(2,1)}, bf16[64,2048]{1,0:T(8,128)(2,1)}, u32[]{:S(2)}, u32[]{:S(2)}) collective-permute-start(bf16[64,2048]{1,0:T(8,128)(2,1)} %get-tuple-element.79), channel_id=1, source_target_pairs={{0,2},{1,3},{2,0},{3,1},{4,6},{5,7},{6,4},{7,5},{8,10},{9,11},{10,... | collective-permute-start | bytes 786440 | tf_op jit(solution)/shard_map/ppermute | solution.py:56
  425.4 90.1 %collective-permute-start.41 = (bf16[64,2048]{1,0:T(8,128)(2,1)}, bf16[64,2048]{1,0:T(8,128)(2,1)}, u32[]{:S(2)}, u32[]{:S(2)}) collective-permute-start(bf16[64,2048]{1,0:T(8,128)(2,1)} %get-tuple-element.76), channel_id=1, source_target_pairs={{0,16},{1,17},{2,18},{3,19},{4,20},{5,21},{6,22},{7,23},{8,24},{9,... | collective-permute-start | bytes 786440 | tf_op jit(solution)/shard_map/ppermute | solution.py:56
  429.6 87.0 %collective-permute-start.46 = (bf16[64,2048]{1,0:T(8,128)(2,1)}, bf16[64,2048]{1,0:T(8,128)(2,1)}, u32[]{:S(2)}, u32[]{:S(2)}) collective-permute-start(bf16[64,2048]{1,0:T(8,128)(2,1)} %get-tuple-element.78), channel_id=1, source_target_pairs={{0,4},{1,5},{2,6},{3,7},{4,0},{5,1},{6,2},{7,3},{8,12},{9,13},{10,... | collective-permute-start | bytes 786440 | tf_op jit(solution)/shard_map/ppermute | solution.py:56
  431.3 60.6 %collective-permute-start.103 = (bf16[64,2048]{1,0:T(8,128)(2,1)}, bf16[64,2048]{1,0:T(8,128)(2,1)}, u32[]{:S(2)}, u32[]{:S(2)}) collective-permute-start(bf16[64,2048]{1,0:T(8,128)(2,1)} %get-tuple-element.51), channel_id=1, source_target_pairs={{0,2},{1,3},{2,0},{3,1},{4,6},{5,7},{6,4},{7,5},{8,10},{9,11},{10,... | collective-permute-start | bytes 786440 | tf_op jit(solution)/shard_map/ppermute | solution.py:56
  595.8 114.6 %collective-permute-start.157 = (bf16[256,6144]{1,0:T(8,128)(2,1)}, bf16[256,6144]{1,0:T(8,128)(2,1)}, u32[]{:S(2)}, u32[]{:S(2)}) collective-permute-start(bf16[256,6144]{1,0:T(8,128)(2,1)} %pad_maximum_fusion.1), channel_id=1, source_target_pairs={{0,1},{1,0},{2,3},{3,2},{4,5},{5,4},{6,7},{7,6},{8,9},{9,8},{10,11... | collective-permute-start | bytes 9437192 | tf_op jit(solution)/shard_map/ppermute | solution.py:56
  663.9 46.8 %collective-permute-start.153 = (bf16[64,2048]{1,0:T(8,128)(2,1)}, bf16[64,2048]{1,0:T(8,128)(2,1)S(1)}, u32[]{:S(2)}, u32[]{:S(2)}) collective-permute-start(bf16[64,2048]{1,0:T(8,128)(2,1)} %get-tuple-element.118), channel_id=1, source_target_pairs={{0,0},{1,4},{2,8},{3,12},{4,16},{5,20},{6,24},{7,28},{8,1},{9,5},{... | collective-permute-start | bytes 786440 | tf_op jit(solution)/shard_map/ppermute | solution.py:56
  665.5 56.3 %collective-permute-start.154 = (bf16[64,2048]{1,0:T(8,128)(2,1)}, bf16[64,2048]{1,0:T(8,128)(2,1)}, u32[]{:S(2)}, u32[]{:S(2)}) collective-permute-start(bf16[64,2048]{1,0:T(8,128)(2,1)} %get-tuple-element.120), channel_id=1, source_target_pairs={{0,3},{1,7},{2,11},{3,15},{4,19},{5,23},{6,27},{7,31},{8,0},{9,4},... | collective-permute-start | bytes 786440 | tf_op jit(solution)/shard_map/ppermute | solution.py:56
  682.6 128.7 %all-to-all-start.1 = ((bf16[32,64,384]{2,1,0:T(8,128)(2,1)}), bf16[32,64,384]{2,1,0:T(8,128)(2,1)}, u32[]{:S(2)}, u32[]{:S(2)}) async-start(bf16[32,64,384]{2,1,0:T(8,128)(2,1)} %bitcast.89), calls=%async_computation.1 | async-start | bytes 3145728 | tf_op jit(solution)/shard_map/all_to_all | solution.py:407
  689.1 55.9 %collective-permute-start.155 = (bf16[64,2048]{1,0:T(8,128)(2,1)}, bf16[64,2048]{1,0:T(8,128)(2,1)S(1)}, u32[]{:S(2)}, u32[]{:S(2)}) collective-permute-start(bf16[64,2048]{1,0:T(8,128)(2,1)} %get-tuple-element.119), channel_id=1, source_target_pairs={{0,2},{1,6},{2,10},{3,14},{4,18},{5,22},{6,26},{7,30},{8,3},{9,7},... | collective-permute-start | bytes 786440 | tf_op jit(solution)/shard_map/ppermute | solution.py:56
  690.8 54.2 %collective-permute-start.156 = (bf16[64,2048]{1,0:T(8,128)(2,1)}, bf16[64,2048]{1,0:T(8,128)(2,1)S(1)}, u32[]{:S(2)}, u32[]{:S(2)}) collective-permute-start(bf16[64,2048]{1,0:T(8,128)(2,1)} %get-tuple-element.121), channel_id=1, source_target_pairs={{0,1},{1,5},{2,9},{3,13},{4,17},{5,21},{6,25},{7,29},{8,2},{9,6},{... | collective-permute-start | bytes 786440 | tf_op jit(solution)/shard_map/ppermute | solution.py:56
  710.4 36.4 %collective-permute-start.146 = (bf16[128,2048]{1,0:T(8,128)(2,1)}, bf16[128,2048]{1,0:T(8,128)(2,1)S(1)}, u32[]{:S(2)}, u32[]{:S(2)}) collective-permute-start(bf16[128,2048]{1,0:T(8,128)(2,1)} %get-tuple-element.42), channel_id=1, source_target_pairs={{0,1},{1,0},{2,3},{3,2},{4,5},{5,4},{6,7},{7,6},{8,9},{9,8},{10,11... | collective-permute-start | bytes 1572872 | tf_op jit(solution)/shard_map/ppermute | solution.py:56
  710.7 36.1 %collective-permute-start.148 = (bf16[128,2048]{1,0:T(8,128)(2,1)}, bf16[128,2048]{1,0:T(8,128)(2,1)S(1)}, u32[]{:S(2)}, u32[]{:S(2)}) collective-permute-start(bf16[128,2048]{1,0:T(8,128)(2,1)} %get-tuple-element.46), channel_id=1, source_target_pairs={{0,4},{1,3},{2,6},{3,1},{4,0},{5,7},{6,2},{7,5},{8,12},{9,11},{10,... | collective-permute-start | bytes 1572872 | tf_op jit(solution)/shard_map/ppermute | solution.py:56
  (210 other events, 2689.2 us)

commit v2 on v1

--- a/solution.py
+++ b/solution.py
@@ -16,7 +16,6 @@
 EPSILON = 1e-06
 NEGATIVE = -1e30
 AXES = ("dp", "seq")
-CHUNKS = 2
 F32 = jnp.float32
 BF16 = jnp.bfloat16
 
@@ -49,87 +48,44 @@
 class Links:
     def __init__(self, dp, seq):
         self.dp, self.seq, self.count = dp, seq, dp * seq
-        self.plane = [1 << b for b in range(1, seq.bit_length() - 1)]
-        self.depth = [seq << b for b in range(dp.bit_length() - 1)]
+        plane = [1 << b for b in range(1, seq.bit_length() - 1)]
+        depth = [seq << b for b in range(dp.bit_length() - 1)]
+        both = lambda bits: [(bit, bit) for bit in bits]
+        self.core = both([1])
+        self.plane = list(zip(plane, plane[::-1]))
+        self.near = both(depth[:1])
+        self.sequence = self.plane + self.core
+        self.tokens = both(depth[1:][::-1]) + self.plane
+        self.every = both([1] + plane + depth)
 
     def send(self, value, target):
         return lax.ppermute(value, AXES, [(i, target(i)) for i in range(self.count)])
 
-    def flip(self, value, mask):
-        return self.send(value, lambda i: i ^ mask)
-
-    def order(self, index):
-        return self.plane if index % 2 == 0 else self.plane[::-1]
-
-    def level(self, value, level):
-        return self.send(value, lambda i: i ^ self.order(i)[level])
+    def flip(self, value, level):
+        return self.send(value, lambda i: i ^ level[i % 2])
 
     def slot_masks(self, index):
-        half = self.seq // 2
-
-        def mask(i, slot):
-            return functools.reduce(
-                lambda a, b: a ^ b,
-                [m for level, m in enumerate(self.order(i)) if slot >> level & 1],
-                0,
-            )
-
-        return [mask(index, s) for s in range(half)] + [1 ^ mask(index ^ 1, s) for s in range(half)]
-
-    def seq_gather(self, value):
-        pieces = [value]
-        for slot in range(1, self.seq // 2):
-            level = slot.bit_length() - 1
-            pieces.append(self.level(pieces[slot ^ (1 << level)], level))
-        return pieces + [self.flip(piece, 1) for piece in pieces]
-
-    def seq_scatter(self, parts):
-        half = self.seq // 2
-        terms = [[parts[s], self.flip(parts[s + half], 1)] for s in range(half)]
-        for slot in range(half - 1, 0, -1):
-            level = slot.bit_length() - 1
-            terms[slot ^ (1 << level)].append(self.level(total(terms[slot]).astype(BF16), level))
-        return total(terms[0])
-
-    def tree(self, bits):
-        groups = {bit: bit if bit in self.plane else 0 for bit in bits}
-        load = {group: 0 for group in groups.values()}
-        far = [bit for bit in bits if bit in self.depth[1:]]
-        parent = {}
-        slots = sorted(
-            (sum(bit for k, bit in enumerate(bits) if pick >> k & 1) for pick in range(1, 1 << len(bits))),
-            key=lambda slot: (bin(slot).count("1"), slot),
-        )
-
-        def choices(slot):
-            inside = [bit for bit in bits if slot & bit]
-            near = [bit for bit in inside if bit not in far]
-            return near or [max(inside)]
-
-        for slot in sorted(slots, key=lambda slot: (len({groups[b] for b in choices(slot)}), slot)):
-            bit = min(choices(slot), key=lambda b: (load[groups[b]], -b))
-            load[groups[bit]] += 1
-            parent[slot] = bit
-        return [(slot, parent[slot]) for slot in slots]
-
-    def gather(self, value, tree):
-        pieces = {0: value}
-        for slot, bit in tree:
-            pieces[slot] = self.flip(pieces[slot ^ bit], bit)
-        return [pieces[slot] for slot in [0] + [s for s, _ in tree]]
-
-    def scatter(self, parts, tree):
-        terms = {slot: [part] for slot, part in zip([0] + [s for s, _ in tree], parts)}
-        for slot, bit in reversed(tree):
-            terms[slot ^ bit].append(self.flip(total(terms[slot]).astype(BF16), bit))
-        return total(terms[0])
-
-
-def total(terms):
-    result = terms[0].astype(F32)
-    for term in terms[1:]:
-        result = result + term.astype(F32)
-    return result
+        masks = [0]
+        for level in self.plane:
+            masks = masks + [mask ^ level[index % 2] for mask in masks]
+        other = [0]
+        for level in self.plane:
+            other = other + [mask ^ level[(index + 1) % 2] for mask in other]
+        return masks + [mask ^ 1 for mask in other]
+
+    def gather(self, value, levels):
+        for level in levels:
+            value = jnp.concatenate([value, self.flip(value, level)], axis=0)
+        return value
+
+    def scatter(self, kept, sent, levels):
+        for level in levels[::-1]:
+            got = self.flip(sent, level)
+            half = kept.shape[0] // 2
+            if level is levels[0]:
+                return kept.astype(F32) + got.astype(F32)
+            sent = (kept[half:].astype(F32) + got[half:].astype(F32)).astype(BF16)
+            kept = kept[:half].astype(F32) + got[:half].astype(F32)
 
 
 def attend_kernel(q_ref, k_ref, v_ref, place_ref, start_ref, key_place_ref, o_ref, lse_ref):
@@ -317,7 +273,7 @@
 
     inputs = layer_input.astype(F32).reshape(tokens, D)
     normed = normalize(inputs, attention_gain).astype(BF16)
-    normed_all = jnp.concatenate(links.seq_gather(normed), axis=0)
+    normed_all = links.gather(normed, links.sequence)
     joined = nn(normed_all, w_in)
     whole = normed_all.shape[0]
 
@@ -333,60 +289,52 @@
     query, keys, values = prepare(joined, query_gain, key_gain)
     query, keys, values = query.astype(BF16), keys.astype(BF16), values.astype(BF16)
     attended, lse = attend(query, keys, values, place, start, length)
-    branch = links.seq_scatter(split(nn(attended, w_out).astype(BF16), seq))
+    middle = whole // 2
+    sent = nn(attended[middle:], w_out).astype(BF16)
+    branch = links.scatter(nn(attended[:middle], w_out), sent, links.sequence)
     resid = inputs + branch
     normed_feed = normalize(resid, feed_gain).astype(BF16)
 
-    tree = links.tree(links.plane + links.depth)
-    other = links.flip(feed_weight, 1)
+    near = links.flip(feed_weight, links.near[0])
+    shares = [feed_weight, near, links.flip(feed_weight, links.core[0]), links.flip(near, links.core[0])]
     gate_up = jnp.concatenate(
-        [feed_weight[:, :D], other[:, :D], feed_weight[:, D : 2 * D], other[:, D : 2 * D]], axis=0
-    )
-    down = jnp.concatenate([feed_weight[:, 2 * D :], other[:, 2 * D :]], axis=0)
+        [share[:, :D] for share in shares] + [share[:, D : 2 * D] for share in shares], axis=0
+    )
+    down = jnp.concatenate([share[:, 2 * D :] for share in shares], axis=0)
+    units = down.shape[0]
     slope_out = cotangent.reshape(tokens, D)
-    slots = len(tree) + 1
-    chunked = []
-    for low, slope in zip(split(normed_feed, CHUNKS), split(slope_out, CHUNKS)):
-        low_all = jnp.concatenate(links.gather(low, tree), axis=0)
-        slope_all = jnp.concatenate(links.gather(slope, tree), axis=0)
-        hidden, slope_both = feed(low_all, slope_all, gate_up, down)
-        chunked.append((low_all, slope_all, hidden, slope_both))
-    slope_normed = jnp.concatenate(
-        [
-            links.scatter(split(nn(slope_both, gate_up).astype(BF16), slots), tree)
-            for _, _, _, slope_both in chunked
-        ],
-        axis=0,
-    )
+    first_levels, last_level = links.tokens[:-1], links.tokens[-1]
+    slope_first_half = links.gather(slope_out, first_levels)
+    slope_last_half = links.flip(slope_first_half, last_level)
+    low_first = links.gather(normed_feed, first_levels)
+    low_last = links.flip(low_first, last_level)
+    hidden_first, both_first = feed(low_first, slope_first_half, gate_up, down)
+    hidden_last, both_last = feed(low_last, slope_last_half, gate_up, down)
+    sent = nn(both_last, gate_up).astype(BF16)
+    slope_normed = links.scatter(nn(both_first, gate_up), sent, links.tokens)
     unused, norm_pull = jax.vjp(normalize, resid, feed_gain)
     slope_resid, feed_gain_part = norm_pull(slope_normed)
     slope_resid = slope_resid + slope_out.astype(F32)
     slope_branch = slope_resid.astype(BF16)
 
-    mixed = jnp.concatenate(
-        [
-            links.scatter(split(nn(hidden, down).astype(BF16), slots), tree)
-            for _, _, hidden, _ in chunked
-        ],
-        axis=0,
+    grad_both = tn(both_first, low_first) + tn(both_last, low_last)
+    grad_down = tn(hidden_first, slope_first_half) + tn(hidden_last, slope_last_half)
+    parts = []
+    for part in (grad_both[:units], grad_both[units:], grad_down):
+        parts.append(
+            links.scatter(part[: units // 2], part[units // 2 :].astype(BF16), links.near + links.core)
+        )
+    feed_weight_gradient = jnp.concatenate(parts, axis=1)
+
+    hidden_first, hidden_last, slope_branch = lax.optimization_barrier(
+        (hidden_first, hidden_last, slope_branch)
+    )
+    mixed = links.scatter(
+        nn(hidden_first, down), nn(hidden_last, down).astype(BF16), links.tokens
     )
     layer_output = (resid + mixed).astype(BF16).reshape(batch, length, D)
 
-    low_all, slope_all, hidden, slope_both = [
-        jnp.concatenate([chunk[k] for chunk in chunked], axis=0) for k in range(4)
-    ]
-    grad_both = tn(slope_both, low_all)
-    grad_down = tn(hidden, slope_all)
-    units = feed_weight.shape[0]
-    mine = jnp.concatenate(
-        [grad_both[:units], grad_both[2 * units : 3 * units], grad_down[:units]], axis=1
-    )
-    theirs = jnp.concatenate(
-        [grad_both[units : 2 * units], grad_both[3 * units :], grad_down[units:]], axis=1
-    )
-    feed_weight_gradient = mine + links.flip(theirs.astype(BF16), 1).astype(F32)
-
-    slope_branch_all = jnp.concatenate(links.seq_gather(slope_branch), axis=0)
+    slope_branch_all = links.gather(slope_branch, links.sequence)
     slope_low = nt(slope_branch_all, w_out).astype(BF16)
     grad_out = tn(attended, slope_branch_all).astype(BF16)
     grad_out = jnp.concatenate([grad_out, grad_out], axis=0)
@@ -396,14 +344,17 @@
     for m in range(dp):
         pairs = {((i % dp + m) % dp) * seq + i // dp: i for i in range(count)}
         pieces.append(links.send(blocks[m], lambda i, pairs=pairs: pairs[i]))
-    attention_out_gradient = total(pieces)
+    attention_out_gradient = sum(piece.astype(F32) for piece in pieces)
 
     dq, dk, dv = attend_back(query, keys, values, slope_low, lse, place, start, length)
     unused, prepare_pull = jax.vjp(prepare, joined, query_gain, key_gain)
     slope_joined, query_gain_part, key_gain_part = prepare_pull((dq, dk, dv))
     slope_joined = slope_joined.astype(BF16)
-    slope_first = links.seq_scatter(split(nt(slope_joined, w_in).astype(BF16), seq))
-    grad_in = tn(normed_all, slope_joined).astype(BF16).reshape(count, rows, columns)
+    grad_in = tn(normed_all, slope_joined)
+    attention_gain_part = jnp.sum(grad_in * w_in.astype(F32), axis=1) / attention_gain
+    grad_in = grad_in.astype(BF16).reshape(count, rows, columns)
+    sent = nt(slope_joined[middle:], w_in).astype(BF16)
+    slope_first = links.scatter(nt(slope_joined[:middle], w_in), sent, links.sequence)
     grad_in = lax.all_to_all(grad_in, AXES, 0, 0, tiled=True).astype(F32)
     grad_in = jnp.sum(grad_in.reshape(dp, seq, rows, columns), axis=0)
     split_key = q_heads * HEAD_DIM
@@ -422,12 +373,14 @@
         ],
         axis=1,
     )
-    unused, first_pull = jax.vjp(normalize, inputs, attention_gain)
-    slope_inputs, attention_gain_part = first_pull(slope_first)
+    unused, first_pull = jax.vjp(lambda v: normalize(v, attention_gain), inputs)
+    (slope_inputs,) = first_pull(slope_first)
     input_gradient = (slope_resid + slope_inputs).astype(BF16).reshape(batch, length, D)
-    gains = lax.psum(
-        jnp.concatenate([attention_gain_part, query_gain_part, key_gain_part, feed_gain_part]), AXES
-    )
+    gains = jnp.concatenate([attention_gain_part, query_gain_part, key_gain_part, feed_gain_part])
+    gains = gains.reshape(-1, 2 * HEAD_DIM)
+    for level in links.every:
+        gains = gains + links.flip(gains, level)
+    gains = gains.reshape(-1)
     cut = [D, D + HEAD_DIM, D + 2 * HEAD_DIM]
     return (
         layer_output,

time: 818 us -> 669 us (0.82); the launches traced: 815 us -> 657 us
  starting transfers between devices: 234 us -> 105 us
  blocking collectives: 57.8 us -> 0 us
  matrix products: 79.1 us -> 120 us
  local copies, waits for them, and re-layouts: 94.9 us -> 65.1 us
  other arithmetic: 56.5 us -> 70.7 us
    ppermute x158 -> x46, starting transfers between devices: 223 us -> 96.2 us  [send(): lax.ppermute(value, AXES, [(i, target(i)) for i in range(self.count)])]
    psum x1 -> x0, blocking collectives: 57.8 us -> none  [on_device(): lax.psum(jnp.concatenate([attention_gain_part, query_gain_part, key_gain_...]
    unnamed x259 -> x191, local copies, waits for them, and re-layouts: 69.1 us -> 32.3 us
    dot_general x6 -> x7, matrix products: 22.9 us -> 37.7 us  [nn(): return jnp.dot(left, right, preferred_element_type=F32)]
    dot_general x6 -> x7, matrix products: 26.3 us -> 40.2 us  [nt(): lax.dot_general(left, right, (((1,), (1,)), ((), ())), preferred_element_...]
    dot_general x4 -> x6, matrix products: 29.9 us -> 42.4 us  [tn(): lax.dot_general(left, right, (((0,), (0,)), ((), ())), preferred_element_...]
    convert_element_type x20 -> x13, other arithmetic: 10.4 us -> 21.3 us  [the longest x10 18.3 us: scatter(): sent = (kept[half:].astype(F32) + got[half:].astype(F32)).astype(BF16)]
    concatenate x1 -> x9, other arithmetic: 1.76 us -> 10 us  [the longest x8 6.99 us: gather(): value = jnp.concatenate([value, self.flip(value, level)], axis=0)]
  transfers between devices with their start and end apart: 160 -> 48, of which waited for: 60 -> 21; matrix products, arithmetic and copies ran while one was open for 26% -> 34% of each run, Pallas kernels for 5% -> 6%
where the time goes in v2:
time: 669 us; the launch traced here: 657 us
  waiting for transfers between devices  254 us (38%)
  matrix products  120 us (18%)
  starting transfers between devices  105 us (16%)
  other arithmetic  70.7 us (11%)
  local copies, waits for them, and re-layouts  65.1 us (10%)
  Pallas kernels  38.9 us (6%)
    ppermute x46, waiting for transfers between devices, send(): lax.ppermute(value, AXES, [(i, target(i)) for i in range(self.count)])  254 us
    ppermute x46, starting transfers between devices, send(): lax.ppermute(value, AXES, [(i, target(i)) for i in range(self.count)])  96.2 us
    dot_general x6, matrix products, tn(): lax.dot_general(left, right, (((0,), (0,)), ((), ())), preferred_element_...  42.4 us
    dot_general x7, matrix products, nt(): lax.dot_general(left, right, (((1,), (1,)), ((), ())), preferred_element_...  40.2 us
    dot_general x7, matrix products, nn(): return jnp.dot(left, right, preferred_element_type=F32)  37.7 us
    unnamed x191, local copies, waits for them, and re-layouts  32.3 us
    pallas_call x1, Pallas kernels, attend_back(): pl.pallas_call(attend_back_kernel, grid=(length // block,), in_specs=[byh...  23.5 us
    convert_element_type x10, other arithmetic, scatter(): sent = (kept[half:].astype(F32) + got[half:].astype(F32)).astype(BF16)  18.3 us
  transfers between devices with their start and end apart: 48, of which 21 were waited for; matrix products, arithmetic and copies ran while one was open for 34% of the time, Pallas kernels for 6%

profile of v2, /device:TPU:0, one launch (start us, length us, event | category | flops | bytes accessed | tf_op | source)
XLA Modules:
  0.0 656.6 jit_solution(4733476965052426646)
XLA Ops:
  37.4 13.7 %collective-permute-done.1 = bf16[256,2048]{1,0:T(8,128)(2,1)} collective-permute-done((bf16[256,2048]{1,0:T(8,128)(2,1)}, bf16[256,2048]{1,0:T(8,128)(2,1)}, u32[]{:S(2)}, u32[]{:S(2)}) %collective-permute-start.1) | collective-permute-done | bytes 1048608 | tf_op jit(solution)/shard_map/ppermute | solution.py:62
  56.5 21.1 %collective-permute-start.12 = (bf16[256,6144]{1,0:T(8,128)(2,1)}, bf16[256,6144]{1,0:T(8,128)(2,1)}, u32[]{:S(2)}, u32[]{:S(2)}) collective-permute-start(bf16[256,6144]{1,0:T(8,128)(2,1)} %param.19), channel_id=1, source_target_pairs={{0,8},{1,9},{2,10},{3,11},{4,12},{5,13},{6,14},{7,15},{8,0},{9,1},... | collective-permute-start | bytes 9437192 | tf_op jit(solution)/shard_map/ppermute | solution.py:62
  105.6 15.4 %attend.1 = (bf16[1024,256]{1,0:T(8,128)(2,1)}, f32[1024,4]{1,0:T(8,128)}) custom-call(bf16[4,1024,64]{2,1,0:T(8,128)(2,1)} %maximum_bitcast_fusion.q_ref, bf16[1024,64]{1,0:T(8,128)(2,1)} %pad_maximum_fusion.20.k_ref, bf16[1024,64]{1,0:T(8,128)(2,1)} %copy.115.v_ref, s32[1024,1]{1,0:T(8,128)} %copy.98.place_ref, s32[1024,1]{1,0:T(8,128)} %copy.99.start_ref, ...), custom_call_target="tpu_custom_call" | custom-call | flops 4294967296 | bytes 2097152 | tf_op jit(solution)/shard_map/attend/pallas_call | solution.py:139
  130.4 23.4 %collective-permute-done.16 = bf16[128,2048]{1,0:T(8,128)(2,1)S(1)} collective-permute-done((bf16[128,2048]{1,0:T(8,128)(2,1)S(1)}, bf16[128,2048]{1,0:T(8,128)(2,1)S(1)}, u32[]{:S(2)}, u32[]{:S(2)}) %collective-permute-start.16) | collective-permute-done | bytes 524320 | tf_op jit(solution)/shard_map/ppermute | solution.py:62
  154.9 7.5 %collective-permute-start.14 = (bf16[256,6144]{1,0:T(8,128)(2,1)}, bf16[256,6144]{1,0:T(8,128)(2,1)}, u32[]{:S(2)}, u32[]{:S(2)}) collective-permute-start(bf16[256,6144]{1,0:T(8,128)(2,1)} %collective-permute-done.12), channel_id=1, source_target_pairs={{0,1},{1,0},{2,3},{3,2},{4,5},{5,4},{6,7},{7,6},{8,9},{9,8},{10,11... | collective-permute-start | bytes 9437192 | tf_op jit(solution)/shard_map/ppermute | solution.py:62
  172.2 10.7 %collective-permute-start.18 = (bf16[512,2048]{1,0:T(8,128)(2,1)S(1)}, bf16[512,2048]{1,0:T(8,128)(2,1)S(1)}, u32[]{:S(2)}, u32[]{:S(2)}) collective-permute-start(bf16[512,2048]{1,0:T(8,128)(2,1)S(1)} %pad_maximum_fusion.5), channel_id=1, source_target_pairs={{0,4},{1,3},{2,6},{3,1},{4,0},{5,7},{6,2},{7,5},{8,12},{9,11},{10,... | collective-permute-start | bytes 6291464 | tf_op jit(solution)/shard_map/ppermute | solution.py:62
  189.1 12.0 %collective-permute-done.9 = bf16[128,2048]{1,0:T(8,128)(2,1)S(1)} collective-permute-done((bf16[128,2048]{1,0:T(8,128)(2,1)S(1)}, bf16[128,2048]{1,0:T(8,128)(2,1)S(1)}, u32[]{:S(2)}, u32[]{:S(2)}) %collective-permute-start.9) | collective-permute-done | bytes 524320 | tf_op jit(solution)/shard_map/ppermute | solution.py:62
  205.5 22.1 %collective-permute-done.10 = bf16[128,2048]{1,0:T(8,128)(2,1)S(1)} collective-permute-done((bf16[128,2048]{1,0:T(8,128)(2,1)S(1)}, bf16[128,2048]{1,0:T(8,128)(2,1)S(1)}, u32[]{:S(2)}, u32[]{:S(2)}) %collective-permute-start.10) | collective-permute-done | bytes 524320 | tf_op jit(solution)/shard_map/ppermute | solution.py:62
  232.5 10.0 %collective-permute-done.11 = bf16[256,2048]{1,0:T(8,128)(2,1)S(1)} collective-permute-done((bf16[256,2048]{1,0:T(8,128)(2,1)S(1)}, bf16[256,2048]{1,0:T(8,128)(2,1)S(1)}, u32[]{:S(2)}, u32[]{:S(2)}) %collective-permute-start.11) | collective-permute-done | bytes 1048608 | tf_op jit(solution)/shard_map/ppermute | solution.py:62
  243.5 10.6 %fusion.78 = f32[512,2048]{1,0:T(8,128)} fusion(bf16[2048,2048]{1,0:T(8,128)(2,1)} %copy-done.54, bf16[256,2048]{1,0:T(8,128)(2,1)S(1)} %collective-permute-done.11, bf16[128,2048]{1,0:T(8,128)(2,1)S(1)} %collective-permute-done.10, bf16[128,2048]{1,0:T(8,128)(2,1)S(1)} %multiply_convert_fusion.6), kind=kOutput, calls=%fused_computation.208 | convolution fusion | flops 4301258752 | bytes 14680064 | tf_op jit(solution)/shard_map/dot_general | solution.py:24
  261.1 7.7 %collective-permute-done.15 = bf16[512,2048]{1,0:T(8,128)(2,1)S(1)} collective-permute-done((bf16[512,2048]{1,0:T(8,128)(2,1)S(1)}, bf16[512,2048]{1,0:T(8,128)(2,1)S(1)}, u32[]{:S(2)}, u32[]{:S(2)}) %collective-permute-start.15) | collective-permute-done | bytes 2097184 | tf_op jit(solution)/shard_map/ppermute | solution.py:62
  283.0 9.1 %convolution_convert_fusion.3 = bf16[512,2048]{1,0:T(8,128)(2,1)} fusion(bf16[2048,2048]{1,0:T(8,128)(2,1)} %copy-done.54, bf16[512,1024]{1,0:T(8,128)(2,1)S(1)} %get-tuple-element.100, bf16[512,1024]{1,0:T(8,128)(2,1)S(1)} %get-tuple-element.99), kind=kOutput, calls=%fused_computation.12 | convolution fusion | flops 4300210176 | bytes 12582912 | tf_op jit(solution)/shard_map/dot_general | solution.py:28
  292.4 8.6 %fusion.12 = f32[2048,2048]{0,1:T(8,128)} fusion(bf16[512,2048]{1,0:T(8,128)(2,1)S(1)} %collective-permute-done.15, bf16[512,1024]{1,0:T(8,128)(2,1)S(1)} %get-tuple-element.100, bf16[512,1024]{1,0:T(8,128)(2,1)S(1)} %get-tuple-element.99), kind=kOutput, calls=%fused_computation.72 | convolution fusion | flops 4299161600 | bytes 20971520 | tf_op jit(solution)/shard_map/dot_general | solution.py:32
  301.1 19.8 %fusion.92 = (bf16[2048,2048]{0,1:T(8,128)(2,1)}, f32[2048,2048]{0,1:T(8,128)}) fusion(f32[2048,2048]{0,1:T(8,128)} %fusion.12, bf16[256,2048]{1,0:T(8,128)(2,1)} %copy-done.18, bf16[128,2048]{1,0:T(8,128)(2,1)S(1)} %collective-permute-done.10, bf16[128,2048]{1,0:T(8,128)(2,1)S(1)} %multiply_convert_fusion.6, bf16[512,1024]{1,0:T(8,128)(2,1)} %get-tuple-element.102, ...), kind=kOutput, calls=%fused_computation.221 | convolution fusion | flops 4313841664 | bytes 46137344 | tf_op jit(solution)/shard_map/dot_general | solution.py:32
  332.9 10.1 %fusion.13 = f32[512,2048]{1,0:T(8,128)} fusion(bf16[2048,2048]{1,0:T(8,128)(2,1)} %copy-done.54, bf16[512,1024]{1,0:T(8,128)(2,1)S(1)} %copy-done.35, bf16[512,1024]{1,0:T(8,128)(2,1)S(1)} %copy-done.34), kind=kOutput, calls=%fused_computation.73 | convolution fusion | flops 4299161600 | bytes 14680064 | tf_op jit(solution)/shard_map/dot_general | solution.py:28
  363.0 24.8 %collective-permute-done.41 = bf16[256,2048]{0,1:T(8,128)(2,1)} collective-permute-done((bf16[256,2048]{0,1:T(8,128)(2,1)S(1)}, bf16[256,2048]{0,1:T(8,128)(2,1)}, u32[]{:S(2)}, u32[]{:S(2)}) %collective-permute-start.41) | collective-permute-done | bytes 1048608 | tf_op jit(solution)/shard_map/ppermute | solution.py:62
  390.5 19.8 %collective-permute-done.45 = bf16[256,2048]{0,1:T(8,128)(2,1)} collective-permute-done((bf16[256,2048]{0,1:T(8,128)(2,1)}, bf16[256,2048]{0,1:T(8,128)(2,1)}, u32[]{:S(2)}, u32[]{:S(2)}) %collective-permute-start.45) | collective-permute-done | bytes 1048608 | tf_op jit(solution)/shard_map/ppermute | solution.py:62
  421.1 7.3 %collective-permute-done.25 = bf16[128,2048]{1,0:T(8,128)(2,1)S(1)} collective-permute-done((bf16[128,2048]{1,0:T(8,128)(2,1)S(1)}, bf16[128,2048]{1,0:T(8,128)(2,1)S(1)}, u32[]{:S(2)}, u32[]{:S(2)}) %collective-permute-start.25) | collective-permute-done | bytes 524320 | tf_op jit(solution)/shard_map/ppermute | solution.py:62
  435.1 22.8 %collective-permute-done.26 = bf16[256,2048]{1,0:T(8,128)(2,1)S(1)} collective-permute-done((bf16[256,2048]{1,0:T(8,128)(2,1)S(1)}, bf16[256,2048]{1,0:T(8,128)(2,1)S(1)}, u32[]{:S(2)}, u32[]{:S(2)}) %collective-permute-start.26) | collective-permute-done | bytes 1048608 | tf_op jit(solution)/shard_map/ppermute | solution.py:62
  486.5 23.5 %attend_back.1 = (f32[4,1024,64]{2,1,0:T(8,128)}, f32[1024,64]{1,0:T(8,128)}, f32[1024,64]{1,0:T(8,128)}) custom-call(bf16[4,1024,64]{2,1,0:T(8,128)(2,1)} %maximum_bitcast_fusion.q_ref, bf16[1024,64]{1,0:T(8,128)(2,1)} %pad_maximum_fusion.20.k_ref, bf16[1024,64]{1,0:T(8,128)(2,1)} %copy.115.v_ref, bf16[1024,256]{1,0:T(8,128)(2,1)} %convolution_convert_fusion.5.do_ref, ...), custom_call_target="tpu_custom_call" | custom-call | flops 10737418240 | bytes 4194304 | tf_op jit(solution)/shard_map/attend_back/pallas_call | solution.py:172
  554.5 10.6 %collective-permute-done.34 = f32[33,128]{1,0:T(8,128)S(1)} collective-permute-done((f32[33,128]{1,0:T(8,128)S(1)}, f32[33,128]{1,0:T(8,128)S(1)}, u32[]{:S(2)}, u32[]{:S(2)}) %collective-permute-start.34) | collective-permute-done | bytes 16928 | tf_op jit(solution)/shard_map/ppermute | solution.py:62
  587.4 23.2 %collective-permute-done.38 = bf16[64,2048]{1,0:T(8,128)(2,1)S(1)} collective-permute-done((bf16[64,2048]{1,0:T(8,128)(2,1)S(1)}, bf16[64,2048]{1,0:T(8,128)(2,1)S(1)}, u32[]{:S(2)}, u32[]{:S(2)}) %collective-permute-start.38) | collective-permute-done | bytes 262176 | tf_op jit(solution)/shard_map/ppermute | solution.py:62
  610.5 28.1 %collective-permute-done.37 = bf16[64,2048]{1,0:T(8,128)(2,1)S(1)} collective-permute-done((bf16[64,2048]{1,0:T(8,128)(2,1)S(1)}, bf16[64,2048]{1,0:T(8,128)(2,1)S(1)}, u32[]{:S(2)}, u32[]{:S(2)}) %collective-permute-start.37) | collective-permute-done | bytes 262176 | tf_op jit(solution)/shard_map/ppermute | solution.py:62
  644.3 8.1 %collective-permute-done.30 = bf16[128,2048]{1,0:T(8,128)(2,1)S(1)} collective-permute-done((bf16[128,2048]{1,0:T(8,128)(2,1)S(1)}, bf16[128,2048]{1,0:T(8,128)(2,1)S(1)}, u32[]{:S(2)}, u32[]{:S(2)}) %collective-permute-start.30) | collective-permute-done | bytes 524320 | tf_op jit(solution)/shard_map/ppermute | solution.py:62
  (391 shorter events, 284.0 us)
Async XLA Ops:
  15.1 36.1 %collective-permute-start.1 = (bf16[256,2048]{1,0:T(8,128)(2,1)}, bf16[256,2048]{1,0:T(8,128)(2,1)}, u32[]{:S(2)}, u32[]{:S(2)}) collective-permute-start(bf16[256,2048]{1,0:T(8,128)(2,1)} %pad_maximum_fusion.13), channel_id=1, source_target_pairs={{0,4},{1,3},{2,6},{3,1},{4,0},{5,7},{6,2},{7,5},{8,12},{9,11},{10,... | collective-permute-start | bytes 3145736 | tf_op jit(solution)/shard_map/ppermute | solution.py:62
  19.1 66.2 %all-to-all-start = ((bf16[32,64,384]{2,1,0:T(8,128)(2,1)}), bf16[32,64,384]{2,1,0:T(8,128)(2,1)S(1)}, u32[]{:S(2)}, u32[]{:S(2)}) async-start(bf16[32,64,384]{2,1,0:T(8,128)(2,1)} %bitcast.3), calls=%async_computation | async-start | bytes 3145728 | tf_op jit(solution)/shard_map/all_to_all | solution.py:261
  24.0 32.5 %collective-permute-start.3 = (bf16[64,2048]{1,0:T(8,128)(2,1)}, bf16[64,2048]{1,0:T(8,128)(2,1)S(1)}, u32[]{:S(2)}, u32[]{:S(2)}) collective-permute-start(bf16[64,2048]{1,0:T(8,128)(2,1)} %param.17), channel_id=1, source_target_pairs={{0,24},{1,0},{2,8},{3,16},{4,25},{5,1},{6,9},{7,17},{8,26},{9,2},{... | collective-permute-start | bytes 786440 | tf_op jit(solution)/shard_map/ppermute | solution.py:62
  29.5 48.7 %collective-permute-start.4 = (bf16[64,2048]{1,0:T(8,128)(2,1)}, bf16[64,2048]{1,0:T(8,128)(2,1)S(1)}, u32[]{:S(2)}, u32[]{:S(2)}) collective-permute-start(bf16[64,2048]{1,0:T(8,128)(2,1)} %param.17), channel_id=1, source_target_pairs={{0,16},{1,24},{2,0},{3,8},{4,17},{5,25},{6,1},{7,9},{8,18},{9,26},... | collective-permute-start | bytes 786440 | tf_op jit(solution)/shard_map/ppermute | solution.py:62
  31.1 47.9 %collective-permute-start.5 = (bf16[64,2048]{1,0:T(8,128)(2,1)}, bf16[64,2048]{1,0:T(8,128)(2,1)S(1)}, u32[]{:S(2)}, u32[]{:S(2)}) collective-permute-start(bf16[64,2048]{1,0:T(8,128)(2,1)} %param.17), channel_id=1, source_target_pairs={{0,8},{1,16},{2,24},{3,0},{4,9},{5,17},{6,25},{7,1},{8,10},{9,18},... | collective-permute-start | bytes 786440 | tf_op jit(solution)/shard_map/ppermute | solution.py:62
  33.5 46.3 %collective-permute-start.6 = (bf16[64,2048]{1,0:T(8,128)(2,1)}, bf16[64,2048]{1,0:T(8,128)(2,1)}, u32[]{:S(2)}, u32[]{:S(2)}) collective-permute-start(bf16[64,2048]{1,0:T(8,128)(2,1)} %param.17), channel_id=1, source_target_pairs={{0,0},{1,8},{2,16},{3,24},{4,1},{5,9},{6,17},{7,25},{8,2},{9,10},{... | collective-permute-start | bytes 786440 | tf_op jit(solution)/shard_map/ppermute | solution.py:62
  56.5 98.4 %collective-permute-start.12 = (bf16[256,6144]{1,0:T(8,128)(2,1)}, bf16[256,6144]{1,0:T(8,128)(2,1)}, u32[]{:S(2)}, u32[]{:S(2)}) collective-permute-start(bf16[256,6144]{1,0:T(8,128)(2,1)} %param.19), channel_id=1, source_target_pairs={{0,8},{1,9},{2,10},{3,11},{4,12},{5,13},{6,14},{7,15},{8,0},{9,1},... | collective-permute-start | bytes 9437192 | tf_op jit(solution)/shard_map/ppermute | solution.py:62
  124.5 43.1 %collective-permute-start.7 = (bf16[512,2048]{1,0:T(8,128)(2,1)}, bf16[512,2048]{1,0:T(8,128)(2,1)}, u32[]{:S(2)}, u32[]{:S(2)}) collective-permute-start(bf16[512,2048]{1,0:T(8,128)(2,1)} %convolution_convert_fusion.1), channel_id=1, source_target_pairs={{0,1},{1,0},{2,3},{3,2},{4,5},{5,4},{6,7},{7,6},{8,9},{9,8},{10,11... | collective-permute-start | bytes 6291464 | tf_op jit(solution)/shard_map/ppermute | solution.py:62
  124.5 59.7 %collective-permute-start.13 = (bf16[256,6144]{1,0:T(8,128)(2,1)}, bf16[256,6144]{1,0:T(8,128)(2,1)}, u32[]{:S(2)}, u32[]{:S(2)}) collective-permute-start(bf16[256,6144]{1,0:T(8,128)(2,1)} %param.19), channel_id=1, source_target_pairs={{0,1},{1,0},{2,3},{3,2},{4,5},{5,4},{6,7},{7,6},{8,9},{9,8},{10,11... | collective-permute-start | bytes 9437192 | tf_op jit(solution)/shard_map/ppermute | solution.py:62
  154.9 31.5 %collective-permute-start.14 = (bf16[256,6144]{1,0:T(8,128)(2,1)}, bf16[256,6144]{1,0:T(8,128)(2,1)}, u32[]{:S(2)}, u32[]{:S(2)}) collective-permute-start(bf16[256,6144]{1,0:T(8,128)(2,1)} %collective-permute-done.12), channel_id=1, source_target_pairs={{0,1},{1,0},{2,3},{3,2},{4,5},{5,4},{6,7},{7,6},{8,9},{9,8},{10,11... | collective-permute-start | bytes 9437192 | tf_op jit(solution)/shard_map/ppermute | solution.py:62
  172.2 103.8 %collective-permute-start.18 = (bf16[512,2048]{1,0:T(8,128)(2,1)S(1)}, bf16[512,2048]{1,0:T(8,128)(2,1)S(1)}, u32[]{:S(2)}, u32[]{:S(2)}) collective-permute-start(bf16[512,2048]{1,0:T(8,128)(2,1)S(1)} %pad_maximum_fusion.5), channel_id=1, source_target_pairs={{0,4},{1,3},{2,6},{3,1},{4,0},{5,7},{6,2},{7,5},{8,12},{9,11},{10,... | collective-permute-start | bytes 6291464 | tf_op jit(solution)/shard_map/ppermute | solution.py:62
  292.1 51.0 %collective-permute-start.19 = (bf16[512,2048]{1,0:T(8,128)(2,1)}, bf16[512,2048]{1,0:T(8,128)(2,1)}, u32[]{:S(2)}, u32[]{:S(2)}) collective-permute-start(bf16[512,2048]{1,0:T(8,128)(2,1)} %convolution_convert_fusion.3), channel_id=1, source_target_pairs={{0,4},{1,3},{2,6},{3,1},{4,0},{5,7},{6,2},{7,5},{8,12},{9,11},{10,... | collective-permute-start | bytes 6291464 | tf_op jit(solution)/shard_map/ppermute | solution.py:62
  350.3 37.4 %collective-permute-start.41 = (bf16[256,2048]{0,1:T(8,128)(2,1)S(1)}, bf16[256,2048]{0,1:T(8,128)(2,1)}, u32[]{:S(2)}, u32[]{:S(2)}) collective-permute-start(bf16[256,2048]{0,1:T(8,128)(2,1)S(1)} %fusion.4), channel_id=1, source_target_pairs={{0,8},{1,9},{2,10},{3,11},{4,12},{5,13},{6,14},{7,15},{8,0},{9,1},... | collective-permute-start | bytes 3145736 | tf_op jit(solution)/shard_map/ppermute | solution.py:62
  353.0 57.2 %collective-permute-start.45 = (bf16[256,2048]{0,1:T(8,128)(2,1)}, bf16[256,2048]{0,1:T(8,128)(2,1)}, u32[]{:S(2)}, u32[]{:S(2)}) collective-permute-start(bf16[256,2048]{0,1:T(8,128)(2,1)} %fusion), channel_id=1, source_target_pairs={{0,8},{1,9},{2,10},{3,11},{4,12},{5,13},{6,14},{7,15},{8,0},{9,1},... | collective-permute-start | bytes 3145736 | tf_op jit(solution)/shard_map/ppermute | solution.py:62
  361.6 52.0 %collective-permute-start.21 = (bf16[128,2048]{1,0:T(8,128)(2,1)S(1)}, bf16[128,2048]{1,0:T(8,128)(2,1)S(1)}, u32[]{:S(2)}, u32[]{:S(2)}) collective-permute-start(bf16[128,2048]{1,0:T(8,128)(2,1)S(1)} %fusion.29), channel_id=1, source_target_pairs={{0,16},{1,17},{2,18},{3,19},{4,20},{5,21},{6,22},{7,23},{8,24},{9,... | collective-permute-start | bytes 1572872 | tf_op jit(solution)/shard_map/ppermute | solution.py:62
  390.4 43.0 %collective-permute-start.43 = (bf16[256,2048]{0,1:T(8,128)(2,1)S(1)}, bf16[256,2048]{0,1:T(8,128)(2,1)}, u32[]{:S(2)}, u32[]{:S(2)}) collective-permute-start(bf16[256,2048]{0,1:T(8,128)(2,1)S(1)} %get-tuple-element.90), channel_id=1, source_target_pairs={{0,8},{1,9},{2,10},{3,11},{4,12},{5,13},{6,14},{7,15},{8,0},{9,1},... | collective-permute-start | bytes 3145736 | tf_op jit(solution)/shard_map/ppermute | solution.py:62
  420.5 39.5 %collective-permute-start.22 = (bf16[512,2048]{1,0:T(8,128)(2,1)}, bf16[512,2048]{1,0:T(8,128)(2,1)S(1)}, u32[]{:S(2)}, u32[]{:S(2)}) collective-permute-start(bf16[512,2048]{1,0:T(8,128)(2,1)} %convolution_convert_fusion), channel_id=1, source_target_pairs={{0,4},{1,3},{2,6},{3,1},{4,0},{5,7},{6,2},{7,5},{8,12},{9,11},{10,... | collective-permute-start | bytes 6291464 | tf_op jit(solution)/shard_map/ppermute | solution.py:62
  478.8 59.6 %collective-permute-start.24 = (bf16[128,2048]{1,0:T(8,128)(2,1)}, bf16[128,2048]{1,0:T(8,128)(2,1)}, u32[]{:S(2)}, u32[]{:S(2)}) collective-permute-start(bf16[128,2048]{1,0:T(8,128)(2,1)} %fusion.25), channel_id=1, source_target_pairs={{0,16},{1,17},{2,18},{3,19},{4,20},{5,21},{6,22},{7,23},{8,24},{9,... | collective-permute-start | bytes 1572872 | tf_op jit(solution)/shard_map/ppermute | solution.py:62
  528.0 51.1 %collective-permute-start.28 = (bf16[512,2048]{1,0:T(8,128)(2,1)}, bf16[512,2048]{1,0:T(8,128)(2,1)}, u32[]{:S(2)}, u32[]{:S(2)}) collective-permute-start(bf16[512,2048]{1,0:T(8,128)(2,1)} %convolution_convert_fusion.2), channel_id=1, source_target_pairs={{0,1},{1,0},{2,3},{3,2},{4,5},{5,4},{6,7},{7,6},{8,9},{9,8},{10,11... | collective-permute-start | bytes 6291464 | tf_op jit(solution)/shard_map/ppermute | solution.py:62
  534.1 105.5 %all-to-all-start.1 = ((bf16[32,64,384]{2,1,0:T(8,128)(2,1)}), bf16[32,64,384]{2,1,0:T(8,128)(2,1)}, u32[]{:S(2)}, u32[]{:S(2)}) async-start(bf16[32,64,384]{2,1,0:T(8,128)(2,1)} %bitcast.93), calls=%async_computation.1 | async-start | bytes 3145728 | tf_op jit(solution)/shard_map/all_to_all | solution.py:358
  572.5 38.1 %collective-permute-start.38 = (bf16[64,2048]{1,0:T(8,128)(2,1)S(1)}, bf16[64,2048]{1,0:T(8,128)(2,1)S(1)}, u32[]{:S(2)}, u32[]{:S(2)}) collective-permute-start(bf16[64,2048]{1,0:T(8,128)(2,1)S(1)} %get-tuple-element.122), channel_id=1, source_target_pairs={{0,2},{1,6},{2,10},{3,14},{4,18},{5,22},{6,26},{7,30},{8,3},{9,7},... | collective-permute-start | bytes 786440 | tf_op jit(solution)/shard_map/ppermute | solution.py:62
  574.1 64.5 %collective-permute-start.37 = (bf16[64,2048]{1,0:T(8,128)(2,1)S(1)}, bf16[64,2048]{1,0:T(8,128)(2,1)S(1)}, u32[]{:S(2)}, u32[]{:S(2)}) collective-permute-start(bf16[64,2048]{1,0:T(8,128)(2,1)S(1)} %get-tuple-element.123), channel_id=1, source_target_pairs={{0,3},{1,7},{2,11},{3,15},{4,19},{5,23},{6,27},{7,31},{8,0},{9,4},... | collective-permute-start | bytes 786440 | tf_op jit(solution)/shard_map/ppermute | solution.py:62
  577.8 60.8 %collective-permute-start.36 = (bf16[64,2048]{1,0:T(8,128)(2,1)S(1)}, bf16[64,2048]{1,0:T(8,128)(2,1)S(1)}, u32[]{:S(2)}, u32[]{:S(2)}) collective-permute-start(bf16[64,2048]{1,0:T(8,128)(2,1)S(1)} %get-tuple-element.121), channel_id=1, source_target_pairs={{0,0},{1,4},{2,8},{3,12},{4,16},{5,20},{6,24},{7,28},{8,1},{9,5},{... | collective-permute-start | bytes 786440 | tf_op jit(solution)/shard_map/ppermute | solution.py:62
  582.2 59.7 %collective-permute-start.29 = (bf16[256,2048]{1,0:T(8,128)(2,1)}, bf16[256,2048]{1,0:T(8,128)(2,1)}, u32[]{:S(2)}, u32[]{:S(2)}) collective-permute-start(bf16[256,2048]{1,0:T(8,128)(2,1)} %get-tuple-element.93), channel_id=1, source_target_pairs={{0,4},{1,3},{2,6},{3,1},{4,0},{5,7},{6,2},{7,5},{8,12},{9,11},{10,... | collective-permute-start | bytes 3145736 | tf_op jit(solution)/shard_map/ppermute | solution.py:62
  (111 other events, 1403.8 us)

commit v3 on v2

--- a/solution.py
+++ b/solution.py
@@ -56,7 +56,7 @@
         self.near = both(depth[:1])
         self.sequence = self.plane + self.core
         self.tokens = both(depth[1:][::-1]) + self.plane
-        self.every = both([1] + plane + depth)
+        self.every = both([1] + depth + plane)
 
     def send(self, value, target):
         return lax.ppermute(value, AXES, [(i, target(i)) for i in range(self.count)])
@@ -86,6 +86,21 @@
                 return kept.astype(F32) + got.astype(F32)
             sent = (kept[half:].astype(F32) + got[half:].astype(F32)).astype(BF16)
             kept = kept[:half].astype(F32) + got[:half].astype(F32)
+
+    def scatter_beside(self, kept, sent, levels, small, small_levels):
+        ends = [1 + (len(small_levels) - 1) * i // (len(levels) - 1) for i in range(len(levels))]
+        done = 0
+        for level, end in zip(levels[::-1], ends):
+            got = self.flip(sent, level)
+            for small_level in small_levels[done:end]:
+                small = small + self.flip(small, small_level)
+            done = end
+            half = kept.shape[0] // 2
+            if level is levels[0]:
+                return kept.astype(F32) + got.astype(F32), small
+            sent = (kept[half:].astype(F32) + got[half:].astype(F32)).astype(BF16)
+            kept = kept[:half].astype(F32) + got[:half].astype(F32)
+            sent, small = lax.optimization_barrier((sent, small))
 
 
 def attend_kernel(q_ref, k_ref, v_ref, place_ref, start_ref, key_place_ref, o_ref, lse_ref):
@@ -288,6 +303,12 @@
 
     query, keys, values = prepare(joined, query_gain, key_gain)
     query, keys, values = query.astype(BF16), keys.astype(BF16), values.astype(BF16)
+    slope_out = cotangent.reshape(tokens, D)
+    first_levels, last_level = links.tokens[:-1], links.tokens[-1]
+    slope_first_half = links.gather(slope_out, first_levels)
+    query, keys, values, slope_first_half = lax.optimization_barrier(
+        (query, keys, values, slope_first_half)
+    )
     attended, lse = attend(query, keys, values, place, start, length)
     middle = whole // 2
     sent = nn(attended[middle:], w_out).astype(BF16)
@@ -302,9 +323,6 @@
     )
     down = jnp.concatenate([share[:, 2 * D :] for share in shares], axis=0)
     units = down.shape[0]
-    slope_out = cotangent.reshape(tokens, D)
-    first_levels, last_level = links.tokens[:-1], links.tokens[-1]
-    slope_first_half = links.gather(slope_out, first_levels)
     slope_last_half = links.flip(slope_first_half, last_level)
     low_first = links.gather(normed_feed, first_levels)
     low_last = links.flip(low_first, last_level)
@@ -344,17 +362,21 @@
     for m in range(dp):
         pairs = {((i % dp + m) % dp) * seq + i // dp: i for i in range(count)}
         pieces.append(links.send(blocks[m], lambda i, pairs=pairs: pairs[i]))
-    attention_out_gradient = sum(piece.astype(F32) for piece in pieces)
 
     dq, dk, dv = attend_back(query, keys, values, slope_low, lse, place, start, length)
     unused, prepare_pull = jax.vjp(prepare, joined, query_gain, key_gain)
     slope_joined, query_gain_part, key_gain_part = prepare_pull((dq, dk, dv))
-    slope_joined = slope_joined.astype(BF16)
+    slope_joined, pieces = lax.optimization_barrier((slope_joined.astype(BF16), pieces))
+    attention_out_gradient = sum(piece.astype(F32) for piece in pieces)
     grad_in = tn(normed_all, slope_joined)
     attention_gain_part = jnp.sum(grad_in * w_in.astype(F32), axis=1) / attention_gain
     grad_in = grad_in.astype(BF16).reshape(count, rows, columns)
     sent = nt(slope_joined[middle:], w_in).astype(BF16)
-    slope_first = links.scatter(nt(slope_joined[:middle], w_in), sent, links.sequence)
+    gains = jnp.concatenate([attention_gain_part, query_gain_part, key_gain_part, feed_gain_part])
+    slope_first, gains = links.scatter_beside(
+        nt(slope_joined[:middle], w_in), sent, links.sequence, gains.reshape(-1, 2 * HEAD_DIM), links.every
+    )
+    gains = gains.reshape(-1)
     grad_in = lax.all_to_all(grad_in, AXES, 0, 0, tiled=True).astype(F32)
     grad_in = jnp.sum(grad_in.reshape(dp, seq, rows, columns), axis=0)
     split_key = q_heads * HEAD_DIM
@@ -376,11 +398,6 @@
     unused, first_pull = jax.vjp(lambda v: normalize(v, attention_gain), inputs)
     (slope_inputs,) = first_pull(slope_first)
     input_gradient = (slope_resid + slope_inputs).astype(BF16).reshape(batch, length, D)
-    gains = jnp.concatenate([attention_gain_part, query_gain_part, key_gain_part, feed_gain_part])
-    gains = gains.reshape(-1, 2 * HEAD_DIM)
-    for level in links.every:
-        gains = gains + links.flip(gains, level)
-    gains = gains.reshape(-1)
     cut = [D, D + HEAD_DIM, D + 2 * HEAD_DIM]
     return (
         layer_output,

time: 669 us -> 648 us (0.969)
  waiting for transfers between devices: 254 us -> 292 us
  starting transfers between devices: 105 us -> 68.6 us
  local copies, waits for them, and re-layouts: 65.1 us -> 48.5 us
  matrix products: 120 us -> 109 us
  other arithmetic: 70.7 us -> 79.5 us
    ppermute x46, starting transfers between devices: 96.2 us -> 52.1 us  [send(): lax.ppermute(value, AXES, [(i, target(i)) for i in range(self.count)])]
    ppermute x46, waiting for transfers between devices: 254 us -> 292 us  [send(): lax.ppermute(value, AXES, [(i, target(i)) for i in range(self.count)])]
    unnamed x191 -> x174, local copies, waits for them, and re-layouts: 32.3 us -> 23.9 us
    all_to_all x1, starting transfers between devices: 4.33 us -> 12.5 us  [on_device(): grad_in = lax.all_to_all(grad_in, AXES, 0, 0, tiled=True).astype(F32)]
    convert_element_type x10 -> x8, other arithmetic: 18.3 us -> 14 us  [scatter(): sent = (kept[half:].astype(F32) + got[half:].astype(F32)).astype(BF16)]
  transfers between devices with their start and end apart: 48 -> 48, of which waited for: 21 -> 21; matrix products, arithmetic and copies ran while one was open for 34% -> 32% of each run, Pallas kernels for 6% -> 6%
where the time goes in v3:
time: 648 us; the launch traced here: 639 us
  waiting for transfers between devices  292 us (45%)
  matrix products  109 us (17%)
  other arithmetic  79.5 us (12%)
  starting transfers between devices  68.6 us (11%)
  local copies, waits for them, and re-layouts  48.5 us (7%)
  Pallas kernels  39.3 us (6%)
    ppermute x46, waiting for transfers between devices, send(): lax.ppermute(value, AXES, [(i, target(i)) for i in range(self.count)])  292 us
    ppermute x46, starting transfers between devices, send(): lax.ppermute(value, AXES, [(i, target(i)) for i in range(self.count)])  52.1 us
    dot_general x6, matrix products, tn(): lax.dot_general(left, right, (((0,), (0,)), ((), ())), preferred_element_...  37.5 us
    dot_general x7, matrix products, nt(): lax.dot_general(left, right, (((1,), (1,)), ((), ())), preferred_element_...  37.3 us
    dot_general x7, matrix products, nn(): return jnp.dot(left, right, preferred_element_type=F32)  33.9 us
    unnamed x174, local copies, waits for them, and re-layouts  23.9 us
    pallas_call x1, Pallas kernels, attend_back(): pl.pallas_call(attend_back_kernel, grid=(length // block,), in_specs=[byh...  23.3 us
    pallas_call x1, Pallas kernels, attend(): pl.pallas_call(attend_kernel, grid=(length // block,), in_specs=[pl.Block...  15.9 us
  transfers between devices with their start and end apart: 48, of which 21 were waited for; matrix products, arithmetic and copies ran while one was open for 32% of the time, Pallas kernels for 6%

profile of v3, /device:TPU:0, one launch (start us, length us, event | category | flops | bytes accessed | tf_op | source)
XLA Modules:
  0.0 639.3 jit_solution(15756759562405016817)
XLA Ops:
  33.6 26.4 %collective-permute-done.1 = bf16[256,2048]{1,0:T(8,128)(2,1)} collective-permute-done((bf16[256,2048]{1,0:T(8,128)(2,1)}, bf16[256,2048]{1,0:T(8,128)(2,1)}, u32[]{:S(2)}, u32[]{:S(2)}) %collective-permute-start.1) | collective-permute-done | bytes 1048608 | tf_op jit(solution)/shard_map/ppermute | solution.py:62
  64.8 28.3 %collective-permute-done.3 = bf16[128,2048]{1,0:T(8,128)(2,1)S(1)} collective-permute-done((bf16[128,2048]{1,0:T(8,128)(2,1)S(1)}, bf16[128,2048]{1,0:T(8,128)(2,1)S(1)}, u32[]{:S(2)}, u32[]{:S(2)}) %collective-permute-start.3) | collective-permute-done | bytes 524320 | tf_op jit(solution)/shard_map/ppermute | solution.py:62
  97.5 10.5 %collective-permute-done.4 = bf16[256,2048]{1,0:T(8,128)(2,1)S(1)} collective-permute-done((bf16[256,2048]{1,0:T(8,128)(2,1)S(1)}, bf16[256,2048]{1,0:T(8,128)(2,1)S(1)}, u32[]{:S(2)}, u32[]{:S(2)}) %collective-permute-start.4) | collective-permute-done | bytes 1048608 | tf_op jit(solution)/shard_map/ppermute | solution.py:62
  128.0 15.9 %attend.1 = (bf16[1024,256]{1,0:T(8,128)(2,1)}, f32[1024,4]{1,0:T(8,128)}) custom-call(bf16[4,1024,64]{2,1,0:T(8,128)(2,1)} %maximum_bitcast_fusion.q_ref, bf16[1024,64]{1,0:T(8,128)(2,1)} %pad_maximum_fusion.20.k_ref, bf16[1024,64]{1,0:T(8,128)(2,1)} %copy.115.v_ref, s32[1024,1]{1,0:T(8,128)} %copy.98.place_ref, s32[1024,1]{1,0:T(8,128)} %copy.99.start_ref, ...), custom_call_target="tpu_custom_call" | custom-call | flops 4294967296 | bytes 2097152 | tf_op jit(solution)/shard_map/attend/pallas_call | solution.py:154
  155.3 10.3 %collective-permute-done.10 = bf16[256,2048]{1,0:T(8,128)(2,1)S(1)} collective-permute-done((bf16[256,2048]{1,0:T(8,128)(2,1)S(1)}, bf16[256,2048]{1,0:T(8,128)(2,1)S(1)}, u32[]{:S(2)}, u32[]{:S(2)}) %collective-permute-start.10) | collective-permute-done | bytes 1048608 | tf_op jit(solution)/shard_map/ppermute | solution.py:62
  166.4 14.3 %collective-permute-done.11 = bf16[128,2048]{1,0:T(8,128)(2,1)S(1)} collective-permute-done((bf16[128,2048]{1,0:T(8,128)(2,1)S(1)}, bf16[128,2048]{1,0:T(8,128)(2,1)S(1)}, u32[]{:S(2)}, u32[]{:S(2)}) %collective-permute-start.11) | collective-permute-done | bytes 524320 | tf_op jit(solution)/shard_map/ppermute | solution.py:62
  183.0 22.6 %collective-permute-done.12 = bf16[128,2048]{1,0:T(8,128)(2,1)S(1)} collective-permute-done((bf16[128,2048]{1,0:T(8,128)(2,1)S(1)}, bf16[128,2048]{1,0:T(8,128)(2,1)S(1)}, u32[]{:S(2)}, u32[]{:S(2)}) %collective-permute-start.12) | collective-permute-done | bytes 524320 | tf_op jit(solution)/shard_map/ppermute | solution.py:62
  209.8 10.8 %collective-permute-done.13 = bf16[256,2048]{1,0:T(8,128)(2,1)S(1)} collective-permute-done((bf16[256,2048]{1,0:T(8,128)(2,1)S(1)}, bf16[256,2048]{1,0:T(8,128)(2,1)S(1)}, u32[]{:S(2)}, u32[]{:S(2)}) %collective-permute-start.13) | collective-permute-done | bytes 1048608 | tf_op jit(solution)/shard_map/ppermute | solution.py:62
  221.2 6.9 %fusion.77 = f32[512,2048]{1,0:T(8,128)S(1)} fusion(bf16[2048,2048]{1,0:T(8,128)(2,1)} %copy-done.54, bf16[256,2048]{1,0:T(8,128)(2,1)S(1)} %collective-permute-done.13, bf16[128,2048]{1,0:T(8,128)(2,1)S(1)} %collective-permute-done.12, bf16[128,2048]{1,0:T(8,128)(2,1)S(1)} %multiply_convert_fusion.6), kind=kOutput, calls=%fused_computation.207 | convolution fusion | flops 4301258752 | bytes 14680064 | tf_op jit(solution)/shard_map/dot_general | solution.py:24
  234.3 10.7 %fusion.13 = f32[512,2048]{1,0:T(8,128)} fusion(bf16[2048,2048]{1,0:T(8,128)(2,1)} %copy-done.54, bf16[512,1024]{1,0:T(8,128)(2,1)S(1)} %get-tuple-element.128, bf16[512,1024]{1,0:T(8,128)(2,1)S(1)} %get-tuple-element.127), kind=kOutput, calls=%fused_computation.73 | convolution fusion | flops 4299161600 | bytes 14680064 | tf_op jit(solution)/shard_map/dot_general | solution.py:28
  247.5 10.6 %fusion.93 = f32[512,2048]{1,0:T(8,128)} fusion(bf16[512,2048]{1,0:T(8,128)(2,1)} %collective-permute-done.17, bf16[2048,2048]{1,0:T(8,128)(2,1)} %copy-done.54), kind=kOutput, calls=%fused_computation.222 | convolution fusion | flops 4294967296 | bytes 14680064 | tf_op jit(solution)/shard_map/dot_general | solution.py:24
  258.2 7.6 %multiply_convert_fusion.1 = (bf16[512,1024]{1,0:T(8,128)(2,1)S(1)}, bf16[512,1024]{1,0:T(8,128)(2,1)S(1)}, bf16[512,1024]{1,0:T(8,128)(2,1)S(1)}) fusion(f32[512,2048]{1,0:T(8,128)} %fusion.93, bf16[512,2048]{1,0:T(8,128)(2,1)S(1)} %collective-permute-done.18, bf16[256,2048]{1,0:T(8,128)(2,1)S(1)} %copy-done.46, ...), kind=kOutput, calls=%fused_computation.57 | convolution fusion | flops 2172125184 | bytes 13631488 | tf_op jit(solution)/shard_map/dot_general | solution.py:24
  265.8 9.6 %convolution_convert_fusion.3 = bf16[512,2048]{1,0:T(8,128)(2,1)} fusion(bf16[2048,2048]{1,0:T(8,128)(2,1)} %copy-done.54, bf16[512,1024]{1,0:T(8,128)(2,1)S(1)} %get-tuple-element.126, bf16[512,1024]{1,0:T(8,128)(2,1)S(1)} %get-tuple-element.125), kind=kOutput, calls=%fused_computation.12 | convolution fusion | flops 4300210176 | bytes 12582912 | tf_op jit(solution)/shard_map/dot_general | solution.py:28
  284.6 9.9 %fusion.12 = f32[2048,2048]{0,1:T(8,128)} fusion(bf16[512,2048]{1,0:T(8,128)(2,1)} %collective-permute-done.17, bf16[512,1024]{1,0:T(8,128)(2,1)S(1)} %get-tuple-element.126, bf16[512,1024]{1,0:T(8,128)(2,1)S(1)} %get-tuple-element.125), kind=kOutput, calls=%fused_computation.72 | convolution fusion | flops 4299161600 | bytes 20971520 | tf_op jit(solution)/shard_map/dot_general | solution.py:32
  294.5 14.9 %fusion.92 = (bf16[2048,2048]{0,1:T(8,128)(2,1)}, f32[2048,2048]{0,1:T(8,128)}) fusion(f32[2048,2048]{0,1:T(8,128)} %fusion.12, bf16[256,2048]{1,0:T(8,128)(2,1)S(1)} %collective-permute-done.13, bf16[128,2048]{1,0:T(8,128)(2,1)S(1)} %collective-permute-done.12, bf16[128,2048]{1,0:T(8,128)(2,1)S(1)} %multiply_convert_fusion.6, ...), kind=kOutput, calls=%fused_computation.221 | convolution fusion | flops 4313841664 | bytes 46137344 | tf_op jit(solution)/shard_map/dot_general | solution.py:32
  320.3 12.6 %collective-permute-done.20 = bf16[256,2048]{1,0:T(8,128)(2,1)} collective-permute-done((bf16[256,2048]{1,0:T(8,128)(2,1)}, bf16[256,2048]{1,0:T(8,128)(2,1)}, u32[]{:S(2)}, u32[]{:S(2)}) %collective-permute-start.20) | collective-permute-done | bytes 1048608 | tf_op jit(solution)/shard_map/ppermute | solution.py:62
  338.1 21.2 %collective-permute-done.21 = bf16[128,2048]{1,0:T(8,128)(2,1)S(1)} collective-permute-done((bf16[128,2048]{1,0:T(8,128)(2,1)S(1)}, bf16[128,2048]{1,0:T(8,128)(2,1)S(1)}, u32[]{:S(2)}, u32[]{:S(2)}) %collective-permute-start.21) | collective-permute-done | bytes 524320 | tf_op jit(solution)/shard_map/ppermute | solution.py:62
  363.6 15.9 %collective-permute-done.41 = bf16[256,2048]{0,1:T(8,128)(2,1)S(1)} collective-permute-done((bf16[256,2048]{0,1:T(8,128)(2,1)S(1)}, bf16[256,2048]{0,1:T(8,128)(2,1)S(1)}, u32[]{:S(2)}, u32[]{:S(2)}) %collective-permute-start.41) | collective-permute-done | bytes 1048608 | tf_op jit(solution)/shard_map/ppermute | solution.py:62
  412.0 9.8 %collective-permute-done.22 = bf16[512,2048]{1,0:T(8,128)(2,1)S(1)} collective-permute-done((bf16[512,2048]{1,0:T(8,128)(2,1)S(1)}, bf16[512,2048]{1,0:T(8,128)(2,1)S(1)}, u32[]{:S(2)}, u32[]{:S(2)}) %collective-permute-start.22) | collective-permute-done | bytes 2097184 | tf_op jit(solution)/shard_map/ppermute | solution.py:62
  430.4 23.3 %attend_back.1 = (f32[4,1024,64]{2,1,0:T(8,128)}, f32[1024,64]{1,0:T(8,128)}, f32[1024,64]{1,0:T(8,128)}) custom-call(bf16[4,1024,64]{2,1,0:T(8,128)(2,1)} %maximum_bitcast_fusion.q_ref, bf16[1024,64]{1,0:T(8,128)(2,1)} %pad_maximum_fusion.20.k_ref, bf16[1024,64]{1,0:T(8,128)(2,1)} %copy.115.v_ref, bf16[1024,256]{1,0:T(8,128)(2,1)} %convolution_convert_fusion.5.do_ref, ...), custom_call_target="tpu_custom_call" | custom-call | flops 10737418240 | bytes 4194304 | tf_op jit(solution)/shard_map/attend_back/pallas_call | solution.py:187
  479.9 50.6 %collective-permute-done.29 = bf16[64,2048]{1,0:T(8,128)(2,1)} collective-permute-done((bf16[64,2048]{1,0:T(8,128)(2,1)S(1)}, bf16[64,2048]{1,0:T(8,128)(2,1)}, u32[]{:S(2)}, u32[]{:S(2)}) %collective-permute-start.29) | collective-permute-done | bytes 262176 | tf_op jit(solution)/shard_map/ppermute | solution.py:62
  538.6 12.5 %all-to-all-start.1 = ((bf16[32,64,384]{2,1,0:T(8,128)(2,1)}), bf16[32,64,384]{2,1,0:T(8,128)(2,1)}, u32[]{:S(2)}, u32[]{:S(2)}) async-start(bf16[32,64,384]{2,1,0:T(8,128)(2,1)} %bitcast.89), calls=%async_computation.1 | async-start | bytes 3145728 | tf_op jit(solution)/shard_map/all_to_all | solution.py:380
  557.0 6.6 %copy.111 = f32[256,6144]{1,0:T(8,128)} copy(f32[256,6144]{0,1:T(8,128)} %pad_maximum_fusion) | data formatting | bytes 12582912
  576.4 34.9 %collective-permute-done.24 = bf16[128,2048]{1,0:T(8,128)(2,1)} collective-permute-done((bf16[128,2048]{1,0:T(8,128)(2,1)}, bf16[128,2048]{1,0:T(8,128)(2,1)}, u32[]{:S(2)}, u32[]{:S(2)}) %collective-permute-start.24) | collective-permute-done | bytes 524320 | tf_op jit(solution)/shard_map/ppermute | solution.py:62
  (373 shorter events, 240.0 us)
Async XLA Ops:
  12.3 50.5 %collective-permute-start.6 = (bf16[64,2048]{1,0:T(8,128)(2,1)}, bf16[64,2048]{1,0:T(8,128)(2,1)}, u32[]{:S(2)}, u32[]{:S(2)}) collective-permute-start(bf16[64,2048]{1,0:T(8,128)(2,1)} %param.17), channel_id=1, source_target_pairs={{0,16},{1,24},{2,0},{3,8},{4,17},{5,25},{6,1},{7,9},{8,18},{9,26},... | collective-permute-start | bytes 786440 | tf_op jit(solution)/shard_map/ppermute | solution.py:62
  13.9 49.9 %collective-permute-start.7 = (bf16[64,2048]{1,0:T(8,128)(2,1)}, bf16[64,2048]{1,0:T(8,128)(2,1)}, u32[]{:S(2)}, u32[]{:S(2)}) collective-permute-start(bf16[64,2048]{1,0:T(8,128)(2,1)} %param.17), channel_id=1, source_target_pairs={{0,8},{1,16},{2,24},{3,0},{4,9},{5,17},{6,25},{7,1},{8,10},{9,18},... | collective-permute-start | bytes 786440 | tf_op jit(solution)/shard_map/ppermute | solution.py:62
  16.1 77.5 %collective-permute-start.8 = (bf16[64,2048]{1,0:T(8,128)(2,1)}, bf16[64,2048]{1,0:T(8,128)(2,1)}, u32[]{:S(2)}, u32[]{:S(2)}) collective-permute-start(bf16[64,2048]{1,0:T(8,128)(2,1)} %param.17), channel_id=1, source_target_pairs={{0,0},{1,8},{2,16},{3,24},{4,1},{5,9},{6,17},{7,25},{8,2},{9,10},{... | collective-permute-start | bytes 786440 | tf_op jit(solution)/shard_map/ppermute | solution.py:62
  21.7 87.9 %all-to-all-start = ((bf16[32,64,384]{2,1,0:T(8,128)(2,1)}), bf16[32,64,384]{2,1,0:T(8,128)(2,1)S(1)}, u32[]{:S(2)}, u32[]{:S(2)}) async-start(bf16[32,64,384]{2,1,0:T(8,128)(2,1)} %bitcast.3), calls=%async_computation | async-start | bytes 3145728 | tf_op jit(solution)/shard_map/all_to_all | solution.py:276
  27.0 33.0 %collective-permute-start.1 = (bf16[256,2048]{1,0:T(8,128)(2,1)}, bf16[256,2048]{1,0:T(8,128)(2,1)}, u32[]{:S(2)}, u32[]{:S(2)}) collective-permute-start(bf16[256,2048]{1,0:T(8,128)(2,1)} %pad_maximum_fusion.13), channel_id=1, source_target_pairs={{0,4},{1,3},{2,6},{3,1},{4,0},{5,7},{6,2},{7,5},{8,12},{9,11},{10,... | collective-permute-start | bytes 3145736 | tf_op jit(solution)/shard_map/ppermute | solution.py:62
  31.1 61.9 %collective-permute-start.3 = (bf16[128,2048]{1,0:T(8,128)(2,1)S(1)}, bf16[128,2048]{1,0:T(8,128)(2,1)S(1)}, u32[]{:S(2)}, u32[]{:S(2)}) collective-permute-start(bf16[128,2048]{1,0:T(8,128)(2,1)S(1)} %bitcast.83), channel_id=1, source_target_pairs={{0,16},{1,17},{2,18},{3,19},{4,20},{5,21},{6,22},{7,23},{8,24},{9,... | collective-permute-start | bytes 1572872 | tf_op jit(solution)/shard_map/ppermute | solution.py:62
  60.1 88.0 %collective-permute-start.14 = (bf16[256,6144]{1,0:T(8,128)(2,1)}, bf16[256,6144]{1,0:T(8,128)(2,1)}, u32[]{:S(2)}, u32[]{:S(2)}) collective-permute-start(bf16[256,6144]{1,0:T(8,128)(2,1)} %param.19), channel_id=1, source_target_pairs={{0,8},{1,9},{2,10},{3,11},{4,12},{5,13},{6,14},{7,15},{8,0},{9,1},... | collective-permute-start | bytes 9437192 | tf_op jit(solution)/shard_map/ppermute | solution.py:62
  62.8 46.8 %collective-permute-start.2 = (bf16[512,2048]{1,0:T(8,128)(2,1)}, bf16[512,2048]{1,0:T(8,128)(2,1)}, u32[]{:S(2)}, u32[]{:S(2)}) collective-permute-start(bf16[512,2048]{1,0:T(8,128)(2,1)} %pad_maximum_fusion.3), channel_id=1, source_target_pairs={{0,1},{1,0},{2,3},{3,2},{4,5},{5,4},{6,7},{7,6},{8,9},{9,8},{10,11... | collective-permute-start | bytes 6291464 | tf_op jit(solution)/shard_map/ppermute | solution.py:62
  154.6 103.5 %collective-permute-start.18 = (bf16[512,2048]{1,0:T(8,128)(2,1)S(1)}, bf16[512,2048]{1,0:T(8,128)(2,1)S(1)}, u32[]{:S(2)}, u32[]{:S(2)}) collective-permute-start(bf16[512,2048]{1,0:T(8,128)(2,1)S(1)} %copy-done.28), channel_id=1, source_target_pairs={{0,4},{1,3},{2,6},{3,1},{4,0},{5,7},{6,2},{7,5},{8,12},{9,11},{10,... | collective-permute-start | bytes 6291464 | tf_op jit(solution)/shard_map/ppermute | solution.py:62
  275.5 39.1 %collective-permute-start.19 = (bf16[512,2048]{1,0:T(8,128)(2,1)}, bf16[512,2048]{1,0:T(8,128)(2,1)}, u32[]{:S(2)}, u32[]{:S(2)}) collective-permute-start(bf16[512,2048]{1,0:T(8,128)(2,1)} %convolution_convert_fusion.3), channel_id=1, source_target_pairs={{0,4},{1,3},{2,6},{3,1},{4,0},{5,7},{6,2},{7,5},{8,12},{9,11},{10,... | collective-permute-start | bytes 6291464 | tf_op jit(solution)/shard_map/ppermute | solution.py:62
  284.6 33.5 %collective-permute-start.44 = (bf16[512,2048]{0,1:T(8,128)(2,1)}, bf16[512,2048]{0,1:T(8,128)(2,1)}, u32[]{:S(2)}, u32[]{:S(2)}) collective-permute-start(bf16[512,2048]{0,1:T(8,128)(2,1)} %slice.624), channel_id=1, source_target_pairs={{0,1},{1,0},{2,3},{3,2},{4,5},{5,4},{6,7},{7,6},{8,9},{9,8},{10,11... | collective-permute-start | bytes 6291464 | tf_op jit(solution)/shard_map/ppermute | solution.py:62
  318.1 45.6 %collective-permute-start.42 = (bf16[512,2048]{0,1:T(8,128)(2,1)}, bf16[512,2048]{0,1:T(8,128)(2,1)S(1)}, u32[]{:S(2)}, u32[]{:S(2)}) collective-permute-start(bf16[512,2048]{0,1:T(8,128)(2,1)} %get-tuple-element.118), channel_id=1, source_target_pairs={{0,1},{1,0},{2,3},{3,2},{4,5},{5,4},{6,7},{7,6},{8,9},{9,8},{10,11... | collective-permute-start | bytes 6291464 | tf_op jit(solution)/shard_map/ppermute | solution.py:62
  320.2 65.3 %collective-permute-start.45 = (bf16[256,2048]{0,1:T(8,128)(2,1)S(1)}, bf16[256,2048]{0,1:T(8,128)(2,1)S(1)}, u32[]{:S(2)}, u32[]{:S(2)}) collective-permute-start(bf16[256,2048]{0,1:T(8,128)(2,1)S(1)} %fusion), channel_id=1, source_target_pairs={{0,8},{1,9},{2,10},{3,11},{4,12},{5,13},{6,14},{7,15},{8,0},{9,1},... | collective-permute-start | bytes 3145736 | tf_op jit(solution)/shard_map/ppermute | solution.py:62
  336.3 43.3 %collective-permute-start.41 = (bf16[256,2048]{0,1:T(8,128)(2,1)S(1)}, bf16[256,2048]{0,1:T(8,128)(2,1)S(1)}, u32[]{:S(2)}, u32[]{:S(2)}) collective-permute-start(bf16[256,2048]{0,1:T(8,128)(2,1)S(1)} %fusion.4), channel_id=1, source_target_pairs={{0,8},{1,9},{2,10},{3,11},{4,12},{5,13},{6,14},{7,15},{8,0},{9,1},... | collective-permute-start | bytes 3145736 | tf_op jit(solution)/shard_map/ppermute | solution.py:62
  392.6 29.2 %collective-permute-start.22 = (bf16[512,2048]{1,0:T(8,128)(2,1)S(1)}, bf16[512,2048]{1,0:T(8,128)(2,1)S(1)}, u32[]{:S(2)}, u32[]{:S(2)}) collective-permute-start(bf16[512,2048]{1,0:T(8,128)(2,1)S(1)} %convolution_convert_fusion), channel_id=1, source_target_pairs={{0,4},{1,3},{2,6},{3,1},{4,0},{5,7},{6,2},{7,5},{8,12},{9,11},{10,... | collective-permute-start | bytes 6291464 | tf_op jit(solution)/shard_map/ppermute | solution.py:62
  424.1 139.5 %collective-permute-start.23 = (bf16[256,2048]{1,0:T(8,128)(2,1)}, bf16[256,2048]{1,0:T(8,128)(2,1)}, u32[]{:S(2)}, u32[]{:S(2)}) collective-permute-start(bf16[256,2048]{1,0:T(8,128)(2,1)} %get-tuple-element.121), channel_id=1, source_target_pairs={{0,2},{1,5},{2,0},{3,7},{4,6},{5,1},{6,4},{7,3},{8,10},{9,13},{10,... | collective-permute-start | bytes 3145736 | tf_op jit(solution)/shard_map/ppermute | solution.py:62
  470.4 60.1 %collective-permute-start.29 = (bf16[64,2048]{1,0:T(8,128)(2,1)S(1)}, bf16[64,2048]{1,0:T(8,128)(2,1)}, u32[]{:S(2)}, u32[]{:S(2)}) collective-permute-start(bf16[64,2048]{1,0:T(8,128)(2,1)S(1)} %get-tuple-element.149), channel_id=1, source_target_pairs={{0,3},{1,7},{2,11},{3,15},{4,19},{5,23},{6,27},{7,31},{8,0},{9,4},... | collective-permute-start | bytes 786440 | tf_op jit(solution)/shard_map/ppermute | solution.py:62
  475.7 54.7 %collective-permute-start.30 = (bf16[64,2048]{1,0:T(8,128)(2,1)S(1)}, bf16[64,2048]{1,0:T(8,128)(2,1)}, u32[]{:S(2)}, u32[]{:S(2)}) collective-permute-start(bf16[64,2048]{1,0:T(8,128)(2,1)S(1)} %get-tuple-element.148), channel_id=1, source_target_pairs={{0,2},{1,6},{2,10},{3,14},{4,18},{5,22},{6,26},{7,30},{8,3},{9,7},... | collective-permute-start | bytes 786440 | tf_op jit(solution)/shard_map/ppermute | solution.py:62
  476.1 54.4 %collective-permute-start.31 = (bf16[64,2048]{1,0:T(8,128)(2,1)S(1)}, bf16[64,2048]{1,0:T(8,128)(2,1)}, u32[]{:S(2)}, u32[]{:S(2)}) collective-permute-start(bf16[64,2048]{1,0:T(8,128)(2,1)S(1)} %get-tuple-element.147), channel_id=1, source_target_pairs={{0,1},{1,5},{2,9},{3,13},{4,17},{5,21},{6,25},{7,29},{8,2},{9,6},{... | collective-permute-start | bytes 786440 | tf_op jit(solution)/shard_map/ppermute | solution.py:62
  533.1 37.0 %collective-permute-start.32 = (bf16[512,2048]{1,0:T(8,128)(2,1)}, bf16[512,2048]{1,0:T(8,128)(2,1)}, u32[]{:S(2)}, u32[]{:S(2)}) collective-permute-start(bf16[512,2048]{1,0:T(8,128)(2,1)} %convolution_convert_fusion.2), channel_id=1, source_target_pairs={{0,1},{1,0},{2,3},{3,2},{4,5},{5,4},{6,7},{7,6},{8,9},{9,8},{10,11... | collective-permute-start | bytes 6291464 | tf_op jit(solution)/shard_map/ppermute | solution.py:62
  538.6 79.6 %all-to-all-start.1 = ((bf16[32,64,384]{2,1,0:T(8,128)(2,1)}), bf16[32,64,384]{2,1,0:T(8,128)(2,1)}, u32[]{:S(2)}, u32[]{:S(2)}) async-start(bf16[32,64,384]{2,1,0:T(8,128)(2,1)} %bitcast.89), calls=%async_computation.1 | async-start | bytes 3145728 | tf_op jit(solution)/shard_map/all_to_all | solution.py:380
  565.8 45.4 %collective-permute-start.24 = (bf16[128,2048]{1,0:T(8,128)(2,1)}, bf16[128,2048]{1,0:T(8,128)(2,1)}, u32[]{:S(2)}, u32[]{:S(2)}) collective-permute-start(bf16[128,2048]{1,0:T(8,128)(2,1)} %fusion.25), channel_id=1, source_target_pairs={{0,16},{1,17},{2,18},{3,19},{4,20},{5,21},{6,22},{7,23},{8,24},{9,... | collective-permute-start | bytes 1572872 | tf_op jit(solution)/shard_map/ppermute | solution.py:62
  573.3 47.5 %collective-permute-start.34 = (bf16[256,2048]{1,0:T(8,128)(2,1)}, bf16[256,2048]{1,0:T(8,128)(2,1)}, u32[]{:S(2)}, u32[]{:S(2)}) collective-permute-start(bf16[256,2048]{1,0:T(8,128)(2,1)} %get-tuple-element.43), channel_id=1, source_target_pairs={{0,4},{1,3},{2,6},{3,1},{4,0},{5,7},{6,2},{7,5},{8,12},{9,11},{10,... | collective-permute-start | bytes 3145736 | tf_op jit(solution)/shard_map/ppermute | solution.py:62
  574.8 38.7 %collective-permute-start.35 = (f32[33,128]{1,0:T(8,128)S(1)}, f32[33,128]{1,0:T(8,128)S(1)}, u32[]{:S(2)}, u32[]{:S(2)}) collective-permute-start(f32[33,128]{1,0:T(8,128)S(1)} %bitcast_add_fusion), channel_id=1, source_target_pairs={{0,8},{1,9},{2,10},{3,11},{4,12},{5,13},{6,14},{7,15},{8,0},{9,1},... | collective-permute-start | bytes 50696 | tf_op jit(solution)/shard_map/ppermute | solution.py:62
  (103 other events, 1700.3 us)

commit v4 on v3

--- a/solution.py
+++ b/solution.py
@@ -350,13 +350,13 @@
     mixed = links.scatter(
         nn(hidden_first, down), nn(hidden_last, down).astype(BF16), links.tokens
     )
-    layer_output = (resid + mixed).astype(BF16).reshape(batch, length, D)
 
     slope_branch_all = links.gather(slope_branch, links.sequence)
     slope_low = nt(slope_branch_all, w_out).astype(BF16)
     grad_out = tn(attended, slope_branch_all).astype(BF16)
     grad_out = jnp.concatenate([grad_out, grad_out], axis=0)
     grad_out = lax.dynamic_slice_in_dim(grad_out, ((here_dp + 1) % dp) * rows, out_rows, 0)
+    grad_out, slope_low = lax.optimization_barrier((grad_out, slope_low))
     blocks = split(grad_out, dp)[::-1]
     pieces = []
     for m in range(dp):
@@ -364,9 +364,11 @@
         pieces.append(links.send(blocks[m], lambda i, pairs=pairs: pairs[i]))
 
     dq, dk, dv = attend_back(query, keys, values, slope_low, lse, place, start, length)
+    dq, dk, dv, pieces = lax.optimization_barrier((dq, dk, dv, pieces))
     unused, prepare_pull = jax.vjp(prepare, joined, query_gain, key_gain)
     slope_joined, query_gain_part, key_gain_part = prepare_pull((dq, dk, dv))
-    slope_joined, pieces = lax.optimization_barrier((slope_joined.astype(BF16), pieces))
+    slope_joined, mixed = lax.optimization_barrier((slope_joined.astype(BF16), mixed))
+    layer_output = (resid + mixed).astype(BF16).reshape(batch, length, D)
     attention_out_gradient = sum(piece.astype(F32) for piece in pieces)
     grad_in = tn(normed_all, slope_joined)
     attention_gain_part = jnp.sum(grad_in * w_in.astype(F32), axis=1) / attention_gain

time: 648 us -> 631 us (0.974)
  waiting for transfers between devices: 292 us -> 256 us
  local copies, waits for them, and re-layouts: 48.5 us -> 63.4 us
  other arithmetic: 79.5 us -> 71.8 us
  starting transfers between devices: 68.6 us -> 76.3 us
    ppermute x46, waiting for transfers between devices: 292 us -> 256 us  [send(): lax.ppermute(value, AXES, [(i, target(i)) for i in range(self.count)])]
    slice x4, local copies, waits for them, and re-layouts: 2.09 us -> 11.6 us  [on_device(): down = jnp.concatenate([share[:, 2 * D:] for share in shares], axis=0)]
    unnamed x174 -> x186, local copies, waits for them, and re-layouts: 23.9 us -> 28.3 us
  transfers between devices with their start and end apart: 48 -> 48, of which waited for: 21 -> 21; matrix products, arithmetic and copies ran while one was open for 32% -> 33% of each run, Pallas kernels for 6% -> 6%
where the time goes in v4:
time: 631 us; the launch traced here: 621 us
  waiting for transfers between devices  256 us (41%)
  matrix products  113 us (18%)
  starting transfers between devices  76.3 us (12%)
  other arithmetic  71.8 us (11%)
  local copies, waits for them, and re-layouts  63.4 us (10%)
  Pallas kernels  38.9 us (6%)
    ppermute x46, waiting for transfers between devices, send(): lax.ppermute(value, AXES, [(i, target(i)) for i in range(self.count)])  256 us
    ppermute x46, starting transfers between devices, send(): lax.ppermute(value, AXES, [(i, target(i)) for i in range(self.count)])  57.6 us
    dot_general x6, matrix products, tn(): lax.dot_general(left, right, (((0,), (0,)), ((), ())), preferred_element_...  41.9 us
    dot_general x7, matrix products, nn(): return jnp.dot(left, right, preferred_element_type=F32)  35.6 us
    dot_general x7, matrix products, nt(): lax.dot_general(left, right, (((1,), (1,)), ((), ())), preferred_element_...  35.3 us
    unnamed x186, local copies, waits for them, and re-layouts  28.3 us
    pallas_call x1, Pallas kernels, attend_back(): pl.pallas_call(attend_back_kernel, grid=(length // block,), in_specs=[byh...  23.2 us
    pallas_call x1, Pallas kernels, attend(): pl.pallas_call(attend_kernel, grid=(length // block,), in_specs=[pl.Block...  15.6 us
  transfers between devices with their start and end apart: 48, of which 21 were waited for; matrix products, arithmetic and copies ran while one was open for 33% of the time, Pallas kernels for 6%

profile of v4, /device:TPU:0, one launch (start us, length us, event | category | flops | bytes accessed | tf_op | source)
XLA Modules:
  0.0 621.2 jit_solution(14806666464233576455)
XLA Ops:
  33.6 26.5 %collective-permute-done.1 = bf16[256,2048]{1,0:T(8,128)(2,1)} collective-permute-done((bf16[256,2048]{1,0:T(8,128)(2,1)}, bf16[256,2048]{1,0:T(8,128)(2,1)}, u32[]{:S(2)}, u32[]{:S(2)}) %collective-permute-start.1) | collective-permute-done | bytes 1048608 | tf_op jit(solution)/shard_map/ppermute | solution.py:62
  64.8 28.3 %collective-permute-done.3 = bf16[128,2048]{1,0:T(8,128)(2,1)S(1)} collective-permute-done((bf16[128,2048]{1,0:T(8,128)(2,1)S(1)}, bf16[128,2048]{1,0:T(8,128)(2,1)S(1)}, u32[]{:S(2)}, u32[]{:S(2)}) %collective-permute-start.3) | collective-permute-done | bytes 524320 | tf_op jit(solution)/shard_map/ppermute | solution.py:62
  97.6 10.5 %collective-permute-done.4 = bf16[256,2048]{1,0:T(8,128)(2,1)S(1)} collective-permute-done((bf16[256,2048]{1,0:T(8,128)(2,1)S(1)}, bf16[256,2048]{1,0:T(8,128)(2,1)S(1)}, u32[]{:S(2)}, u32[]{:S(2)}) %collective-permute-start.4) | collective-permute-done | bytes 1048608 | tf_op jit(solution)/shard_map/ppermute | solution.py:62
  128.0 15.6 %attend.1 = (bf16[1024,256]{1,0:T(8,128)(2,1)}, f32[1024,4]{1,0:T(8,128)}) custom-call(bf16[4,1024,64]{2,1,0:T(8,128)(2,1)} %maximum_bitcast_fusion.q_ref, bf16[1024,64]{1,0:T(8,128)(2,1)} %pad_maximum_fusion.20.k_ref, bf16[1024,64]{1,0:T(8,128)(2,1)} %copy.115.v_ref, s32[1024,1]{1,0:T(8,128)} %copy.98.place_ref, s32[1024,1]{1,0:T(8,128)} %copy.99.start_ref, ...), custom_call_target="tpu_custom_call" | custom-call | flops 4294967296 | bytes 2097152 | tf_op jit(solution)/shard_map/attend/pallas_call | solution.py:154
  171.4 9.8 %collective-permute-done.11 = bf16[128,2048]{1,0:T(8,128)(2,1)S(1)} collective-permute-done((bf16[128,2048]{1,0:T(8,128)(2,1)S(1)}, bf16[128,2048]{1,0:T(8,128)(2,1)S(1)}, u32[]{:S(2)}, u32[]{:S(2)}) %collective-permute-start.11) | collective-permute-done | bytes 524320 | tf_op jit(solution)/shard_map/ppermute | solution.py:62
  185.6 21.6 %collective-permute-done.12 = bf16[128,2048]{1,0:T(8,128)(2,1)S(1)} collective-permute-done((bf16[128,2048]{1,0:T(8,128)(2,1)S(1)}, bf16[128,2048]{1,0:T(8,128)(2,1)S(1)}, u32[]{:S(2)}, u32[]{:S(2)}) %collective-permute-start.12) | collective-permute-done | bytes 524320 | tf_op jit(solution)/shard_map/ppermute | solution.py:62
  213.5 8.7 %collective-permute-done.13 = bf16[256,2048]{1,0:T(8,128)(2,1)S(1)} collective-permute-done((bf16[256,2048]{1,0:T(8,128)(2,1)S(1)}, bf16[256,2048]{1,0:T(8,128)(2,1)S(1)}, u32[]{:S(2)}, u32[]{:S(2)}) %collective-permute-start.13) | collective-permute-done | bytes 1048608 | tf_op jit(solution)/shard_map/ppermute | solution.py:62
  223.0 7.0 %fusion.75 = f32[512,2048]{1,0:T(8,128)S(1)} fusion(bf16[2048,2048]{1,0:T(8,128)(2,1)} %get-tuple-element.156, bf16[256,2048]{1,0:T(8,128)(2,1)S(1)} %collective-permute-done.13, bf16[128,2048]{1,0:T(8,128)(2,1)S(1)} %collective-permute-done.12, bf16[128,2048]{1,0:T(8,128)(2,1)S(1)} %multiply_convert_fusion.6), kind=kOutput, calls=%fused_computation.206 | convolution fusion | flops 4301258752 | bytes 14680064 | tf_op jit(solution)/shard_map/dot_general | solution.py:24
  230.0 8.0 %multiply_convert_fusion.3 = (bf16[512,1024]{1,0:T(8,128)(2,1)}, bf16[512,1024]{1,0:T(8,128)(2,1)}, bf16[512,1024]{1,0:T(8,128)(2,1)S(1)}) fusion(f32[512,2048]{1,0:T(8,128)S(1)} %fusion.75, bf16[512,2048]{1,0:T(8,128)(2,1)S(1)} %copy-done.28, bf16[256,2048]{1,0:T(8,128)(2,1)S(1)} %get-tuple-element.155, bf16[256,2048]{1,0:T(8,128)(2,1)S(1)} %get-tuple-element.153, ...), kind=kOutput, calls=%fused_computation.59 | convolution fusion | flops 2172125184 | bytes 13631488 | tf_op jit(solution)/shard_map/dot_general | solution.py:24
  248.4 7.3 %fusion.91 = f32[512,2048]{1,0:T(8,128)S(1)} fusion(bf16[512,2048]{1,0:T(8,128)(2,1)S(1)} %collective-permute-done.17, bf16[2048,2048]{1,0:T(8,128)(2,1)} %get-tuple-element.156), kind=kOutput, calls=%fused_computation.221 | convolution fusion | flops 4294967296 | bytes 14680064 | tf_op jit(solution)/shard_map/dot_general | solution.py:24
  255.8 7.0 %multiply_convert_fusion.1 = (bf16[512,1024]{1,0:T(8,128)(2,1)S(1)}, bf16[512,1024]{1,0:T(8,128)(2,1)S(1)}, bf16[512,1024]{1,0:T(8,128)(2,1)}) fusion(f32[512,2048]{1,0:T(8,128)S(1)} %fusion.91, bf16[512,2048]{1,0:T(8,128)(2,1)S(1)} %collective-permute-done.18, bf16[256,2048]{1,0:T(8,128)(2,1)S(1)} %get-tuple-element.155, ...), kind=kOutput, calls=%fused_computation.57 | convolution fusion | flops 2172125184 | bytes 13631488 | tf_op jit(solution)/shard_map/dot_general | solution.py:24
  262.8 9.1 %convolution_convert_fusion.3 = bf16[512,2048]{1,0:T(8,128)(2,1)} fusion(bf16[2048,2048]{1,0:T(8,128)(2,1)} %get-tuple-element.156, bf16[512,1024]{1,0:T(8,128)(2,1)S(1)} %get-tuple-element.138, bf16[512,1024]{1,0:T(8,128)(2,1)S(1)} %get-tuple-element.137), kind=kOutput, calls=%fused_computation.12 | convolution fusion | flops 4300210176 | bytes 12582912 | tf_op jit(solution)/shard_map/dot_general | solution.py:28
  272.5 8.3 %fusion.12 = f32[2048,2048]{0,1:T(8,128)} fusion(bf16[512,2048]{1,0:T(8,128)(2,1)S(1)} %collective-permute-done.17, bf16[512,1024]{1,0:T(8,128)(2,1)S(1)} %get-tuple-element.138, bf16[512,1024]{1,0:T(8,128)(2,1)S(1)} %get-tuple-element.137), kind=kOutput, calls=%fused_computation.72 | convolution fusion | flops 4299161600 | bytes 20971520 | tf_op jit(solution)/shard_map/dot_general | solution.py:32
  280.7 15.0 %fusion.90 = (bf16[2048,2048]{0,1:T(8,128)(2,1)}, f32[2048,2048]{0,1:T(8,128)}) fusion(f32[2048,2048]{0,1:T(8,128)} %fusion.12, bf16[256,2048]{1,0:T(8,128)(2,1)S(1)} %collective-permute-done.13, bf16[128,2048]{1,0:T(8,128)(2,1)S(1)} %collective-permute-done.12, bf16[128,2048]{1,0:T(8,128)(2,1)S(1)} %multiply_convert_fusion.6, ...), kind=kOutput, calls=%fused_computation.220 | convolution fusion | flops 4313841664 | bytes 46137344 | tf_op jit(solution)/shard_map/dot_general | solution.py:32
  308.8 10.8 %fusion.13 = f32[512,2048]{1,0:T(8,128)} fusion(bf16[2048,2048]{1,0:T(8,128)(2,1)} %get-tuple-element.156, bf16[512,1024]{1,0:T(8,128)(2,1)} %get-tuple-element.140, bf16[512,1024]{1,0:T(8,128)(2,1)S(1)} %copy-done.37), kind=kOutput, calls=%fused_computation.73 | convolution fusion | flops 4299161600 | bytes 14680064 | tf_op jit(solution)/shard_map/dot_general | solution.py:28
  328.5 9.4 %collective-permute-done.20 = bf16[256,2048]{1,0:T(8,128)(2,1)S(1)} collective-permute-done((bf16[256,2048]{1,0:T(8,128)(2,1)S(1)}, bf16[256,2048]{1,0:T(8,128)(2,1)S(1)}, u32[]{:S(2)}, u32[]{:S(2)}) %collective-permute-start.20) | collective-permute-done | bytes 1048608 | tf_op jit(solution)/shard_map/ppermute | solution.py:62
  338.1 22.7 %collective-permute-done.41 = bf16[256,2048]{0,1:T(8,128)(2,1)} collective-permute-done((bf16[256,2048]{0,1:T(8,128)(2,1)S(1)}, bf16[256,2048]{0,1:T(8,128)(2,1)}, u32[]{:S(2)}, u32[]{:S(2)}) %collective-permute-start.41) | collective-permute-done | bytes 1048608 | tf_op jit(solution)/shard_map/ppermute | solution.py:62
  364.5 16.0 %collective-permute-done.21 = bf16[128,2048]{1,0:T(8,128)(2,1)S(1)} collective-permute-done((bf16[128,2048]{1,0:T(8,128)(2,1)S(1)}, bf16[128,2048]{1,0:T(8,128)(2,1)S(1)}, u32[]{:S(2)}, u32[]{:S(2)}) %collective-permute-start.21) | collective-permute-done | bytes 524320 | tf_op jit(solution)/shard_map/ppermute | solution.py:62
  399.6 28.0 %collective-permute-done.23 = bf16[256,2048]{1,0:T(8,128)(2,1)S(1)} collective-permute-done((bf16[256,2048]{1,0:T(8,128)(2,1)S(1)}, bf16[256,2048]{1,0:T(8,128)(2,1)S(1)}, u32[]{:S(2)}, u32[]{:S(2)}) %collective-permute-start.23) | collective-permute-done | bytes 1048608 | tf_op jit(solution)/shard_map/ppermute | solution.py:62
  433.5 10.0 %collective-permute-done.30 = bf16[256,2048]{1,0:T(8,128)(2,1)S(1)} collective-permute-done((bf16[256,2048]{1,0:T(8,128)(2,1)S(1)}, bf16[256,2048]{1,0:T(8,128)(2,1)S(1)}, u32[]{:S(2)}, u32[]{:S(2)}) %collective-permute-start.30) | collective-permute-done | bytes 1048608 | tf_op jit(solution)/shard_map/ppermute | solution.py:62
  463.3 23.2 %attend_back.1 = (f32[4,1024,64]{2,1,0:T(8,128)}, f32[1024,64]{1,0:T(8,128)}, f32[1024,64]{1,0:T(8,128)}) custom-call(bf16[4,1024,64]{2,1,0:T(8,128)(2,1)} %maximum_bitcast_fusion.q_ref, bf16[1024,64]{1,0:T(8,128)(2,1)} %pad_maximum_fusion.20.k_ref, bf16[1024,64]{1,0:T(8,128)(2,1)} %copy.115.v_ref, bf16[1024,256]{1,0:T(8,128)(2,1)} %convolution_convert_fusion.5.do_ref, ...), custom_call_target="tpu_custom_call" | custom-call | flops 10737418240 | bytes 4194304 | tf_op jit(solution)/shard_map/attend_back/pallas_call | solution.py:187
  486.6 8.3 %collective-permute-done.31 = bf16[128,2048]{1,0:T(8,128)(2,1)} collective-permute-done((bf16[128,2048]{1,0:T(8,128)(2,1)}, bf16[128,2048]{1,0:T(8,128)(2,1)}, u32[]{:S(2)}, u32[]{:S(2)}) %collective-permute-start.31) | collective-permute-done | bytes 524320 | tf_op jit(solution)/shard_map/ppermute | solution.py:62
  497.2 27.5 %collective-permute-done.26 = bf16[64,2048]{1,0:T(8,128)(2,1)} collective-permute-done((bf16[64,2048]{1,0:T(8,128)(2,1)}, bf16[64,2048]{1,0:T(8,128)(2,1)}, u32[]{:S(2)}, u32[]{:S(2)}) %collective-permute-start.26) | collective-permute-done | bytes 262176 | tf_op jit(solution)/shard_map/ppermute | solution.py:62
  546.8 14.7 %all-to-all-start.1 = ((bf16[32,64,384]{2,1,0:T(8,128)(2,1)}), bf16[32,64,384]{2,1,0:T(8,128)(2,1)}, u32[]{:S(2)}, u32[]{:S(2)}) async-start(bf16[32,64,384]{2,1,0:T(8,128)(2,1)} %bitcast.91), calls=%async_computation.1 | async-start | bytes 3145728 | tf_op jit(solution)/shard_map/all_to_all | solution.py:382
  (387 shorter events, 265.6 us)
Async XLA Ops:
  12.3 50.5 %collective-permute-start.6 = (bf16[64,2048]{1,0:T(8,128)(2,1)}, bf16[64,2048]{1,0:T(8,128)(2,1)}, u32[]{:S(2)}, u32[]{:S(2)}) collective-permute-start(bf16[64,2048]{1,0:T(8,128)(2,1)} %param.17), channel_id=1, source_target_pairs={{0,16},{1,24},{2,0},{3,8},{4,17},{5,25},{6,1},{7,9},{8,18},{9,26},... | collective-permute-start | bytes 786440 | tf_op jit(solution)/shard_map/ppermute | solution.py:62
  13.9 49.9 %collective-permute-start.7 = (bf16[64,2048]{1,0:T(8,128)(2,1)}, bf16[64,2048]{1,0:T(8,128)(2,1)}, u32[]{:S(2)}, u32[]{:S(2)}) collective-permute-start(bf16[64,2048]{1,0:T(8,128)(2,1)} %param.17), channel_id=1, source_target_pairs={{0,8},{1,16},{2,24},{3,0},{4,9},{5,17},{6,25},{7,1},{8,10},{9,18},... | collective-permute-start | bytes 786440 | tf_op jit(solution)/shard_map/ppermute | solution.py:62
  16.1 77.5 %collective-permute-start.8 = (bf16[64,2048]{1,0:T(8,128)(2,1)}, bf16[64,2048]{1,0:T(8,128)(2,1)}, u32[]{:S(2)}, u32[]{:S(2)}) collective-permute-start(bf16[64,2048]{1,0:T(8,128)(2,1)} %param.17), channel_id=1, source_target_pairs={{0,0},{1,8},{2,16},{3,24},{4,1},{5,9},{6,17},{7,25},{8,2},{9,10},{... | collective-permute-start | bytes 786440 | tf_op jit(solution)/shard_map/ppermute | solution.py:62
  21.7 88.0 %all-to-all-start = ((bf16[32,64,384]{2,1,0:T(8,128)(2,1)}), bf16[32,64,384]{2,1,0:T(8,128)(2,1)S(1)}, u32[]{:S(2)}, u32[]{:S(2)}) async-start(bf16[32,64,384]{2,1,0:T(8,128)(2,1)} %bitcast.3), calls=%async_computation | async-start | bytes 3145728 | tf_op jit(solution)/shard_map/all_to_all | solution.py:276
  27.0 33.0 %collective-permute-start.1 = (bf16[256,2048]{1,0:T(8,128)(2,1)}, bf16[256,2048]{1,0:T(8,128)(2,1)}, u32[]{:S(2)}, u32[]{:S(2)}) collective-permute-start(bf16[256,2048]{1,0:T(8,128)(2,1)} %pad_maximum_fusion.13), channel_id=1, source_target_pairs={{0,4},{1,3},{2,6},{3,1},{4,0},{5,7},{6,2},{7,5},{8,12},{9,11},{10,... | collective-permute-start | bytes 3145736 | tf_op jit(solution)/shard_map/ppermute | solution.py:62
  31.1 62.0 %collective-permute-start.3 = (bf16[128,2048]{1,0:T(8,128)(2,1)S(1)}, bf16[128,2048]{1,0:T(8,128)(2,1)S(1)}, u32[]{:S(2)}, u32[]{:S(2)}) collective-permute-start(bf16[128,2048]{1,0:T(8,128)(2,1)S(1)} %bitcast.85), channel_id=1, source_target_pairs={{0,16},{1,17},{2,18},{3,19},{4,20},{5,21},{6,22},{7,23},{8,24},{9,... | collective-permute-start | bytes 1572872 | tf_op jit(solution)/shard_map/ppermute | solution.py:62
  60.0 88.0 %collective-permute-start.14 = (bf16[256,6144]{1,0:T(8,128)(2,1)}, bf16[256,6144]{1,0:T(8,128)(2,1)}, u32[]{:S(2)}, u32[]{:S(2)}) collective-permute-start(bf16[256,6144]{1,0:T(8,128)(2,1)} %param.19), channel_id=1, source_target_pairs={{0,8},{1,9},{2,10},{3,11},{4,12},{5,13},{6,14},{7,15},{8,0},{9,1},... | collective-permute-start | bytes 9437192 | tf_op jit(solution)/shard_map/ppermute | solution.py:62
  62.8 46.9 %collective-permute-start.2 = (bf16[512,2048]{1,0:T(8,128)(2,1)}, bf16[512,2048]{1,0:T(8,128)(2,1)}, u32[]{:S(2)}, u32[]{:S(2)}) collective-permute-start(bf16[512,2048]{1,0:T(8,128)(2,1)} %pad_maximum_fusion.3), channel_id=1, source_target_pairs={{0,1},{1,0},{2,3},{3,2},{4,5},{5,4},{6,7},{7,6},{8,9},{9,8},{10,11... | collective-permute-start | bytes 6291464 | tf_op jit(solution)/shard_map/ppermute | solution.py:62
  158.5 97.2 %collective-permute-start.18 = (bf16[512,2048]{1,0:T(8,128)(2,1)S(1)}, bf16[512,2048]{1,0:T(8,128)(2,1)S(1)}, u32[]{:S(2)}, u32[]{:S(2)}) collective-permute-start(bf16[512,2048]{1,0:T(8,128)(2,1)S(1)} %copy-done.28), channel_id=1, source_target_pairs={{0,4},{1,3},{2,6},{3,1},{4,0},{5,7},{6,2},{7,5},{8,12},{9,11},{10,... | collective-permute-start | bytes 6291464 | tf_op jit(solution)/shard_map/ppermute | solution.py:62
  222.3 26.1 %collective-permute-start.17 = (bf16[512,2048]{1,0:T(8,128)(2,1)S(1)}, bf16[512,2048]{1,0:T(8,128)(2,1)S(1)}, u32[]{:S(2)}, u32[]{:S(2)}) collective-permute-start(bf16[512,2048]{1,0:T(8,128)(2,1)S(1)} %pad_maximum_fusion.5), channel_id=1, source_target_pairs={{0,4},{1,3},{2,6},{3,1},{4,0},{5,7},{6,2},{7,5},{8,12},{9,11},{10,... | collective-permute-start | bytes 6291464 | tf_op jit(solution)/shard_map/ppermute | solution.py:62
  271.9 47.7 %collective-permute-start.19 = (bf16[512,2048]{1,0:T(8,128)(2,1)}, bf16[512,2048]{1,0:T(8,128)(2,1)}, u32[]{:S(2)}, u32[]{:S(2)}) collective-permute-start(bf16[512,2048]{1,0:T(8,128)(2,1)} %convolution_convert_fusion.3), channel_id=1, source_target_pairs={{0,4},{1,3},{2,6},{3,1},{4,0},{5,7},{6,2},{7,5},{8,12},{9,11},{10,... | collective-permute-start | bytes 6291464 | tf_op jit(solution)/shard_map/ppermute | solution.py:62
  323.8 37.1 %collective-permute-start.41 = (bf16[256,2048]{0,1:T(8,128)(2,1)S(1)}, bf16[256,2048]{0,1:T(8,128)(2,1)}, u32[]{:S(2)}, u32[]{:S(2)}) collective-permute-start(bf16[256,2048]{0,1:T(8,128)(2,1)S(1)} %fusion.4), channel_id=1, source_target_pairs={{0,8},{1,9},{2,10},{3,11},{4,12},{5,13},{6,14},{7,15},{8,0},{9,1},... | collective-permute-start | bytes 3145736 | tf_op jit(solution)/shard_map/ppermute | solution.py:62
  326.5 65.0 %collective-permute-start.45 = (bf16[256,2048]{0,1:T(8,128)(2,1)}, bf16[256,2048]{0,1:T(8,128)(2,1)}, u32[]{:S(2)}, u32[]{:S(2)}) collective-permute-start(bf16[256,2048]{0,1:T(8,128)(2,1)} %fusion), channel_id=1, source_target_pairs={{0,8},{1,9},{2,10},{3,11},{4,12},{5,13},{6,14},{7,15},{8,0},{9,1},... | collective-permute-start | bytes 3145736 | tf_op jit(solution)/shard_map/ppermute | solution.py:62
  338.0 42.5 %collective-permute-start.21 = (bf16[128,2048]{1,0:T(8,128)(2,1)S(1)}, bf16[128,2048]{1,0:T(8,128)(2,1)S(1)}, u32[]{:S(2)}, u32[]{:S(2)}) collective-permute-start(bf16[128,2048]{1,0:T(8,128)(2,1)S(1)} %fusion.27), channel_id=1, source_target_pairs={{0,16},{1,17},{2,18},{3,19},{4,20},{5,21},{6,22},{7,23},{8,24},{9,... | collective-permute-start | bytes 1572872 | tf_op jit(solution)/shard_map/ppermute | solution.py:62
  364.5 65.8 %collective-permute-start.43 = (bf16[256,2048]{0,1:T(8,128)(2,1)}, bf16[256,2048]{0,1:T(8,128)(2,1)}, u32[]{:S(2)}, u32[]{:S(2)}) collective-permute-start(bf16[256,2048]{0,1:T(8,128)(2,1)} %get-tuple-element.128), channel_id=1, source_target_pairs={{0,8},{1,9},{2,10},{3,11},{4,12},{5,13},{6,14},{7,15},{8,0},{9,1},... | collective-permute-start | bytes 3145736 | tf_op jit(solution)/shard_map/ppermute | solution.py:62
  390.1 37.8 %collective-permute-start.29 = (bf16[512,2048]{1,0:T(8,128)(2,1)}, bf16[512,2048]{1,0:T(8,128)(2,1)S(1)}, u32[]{:S(2)}, u32[]{:S(2)}) collective-permute-start(bf16[512,2048]{1,0:T(8,128)(2,1)} %convolution_convert_fusion), channel_id=1, source_target_pairs={{0,4},{1,3},{2,6},{3,1},{4,0},{5,7},{6,2},{7,5},{8,12},{9,11},{10,... | collective-permute-start | bytes 6291464 | tf_op jit(solution)/shard_map/ppermute | solution.py:62
  395.1 32.4 %collective-permute-start.23 = (bf16[256,2048]{1,0:T(8,128)(2,1)S(1)}, bf16[256,2048]{1,0:T(8,128)(2,1)S(1)}, u32[]{:S(2)}, u32[]{:S(2)}) collective-permute-start(bf16[256,2048]{1,0:T(8,128)(2,1)S(1)} %pad_maximum_fusion.16), channel_id=1, source_target_pairs={{0,4},{1,3},{2,6},{3,1},{4,0},{5,7},{6,2},{7,5},{8,12},{9,11},{10,... | collective-permute-start | bytes 3145736 | tf_op jit(solution)/shard_map/ppermute | solution.py:62
  444.6 50.3 %collective-permute-start.31 = (bf16[128,2048]{1,0:T(8,128)(2,1)}, bf16[128,2048]{1,0:T(8,128)(2,1)}, u32[]{:S(2)}, u32[]{:S(2)}) collective-permute-start(bf16[128,2048]{1,0:T(8,128)(2,1)} %fusion.25), channel_id=1, source_target_pairs={{0,16},{1,17},{2,18},{3,19},{4,20},{5,21},{6,22},{7,23},{8,24},{9,... | collective-permute-start | bytes 1572872 | tf_op jit(solution)/shard_map/ppermute | solution.py:62
  453.9 43.4 %collective-permute-start.25 = (bf16[64,2048]{1,0:T(8,128)(2,1)}, bf16[64,2048]{1,0:T(8,128)(2,1)S(1)}, u32[]{:S(2)}, u32[]{:S(2)}) collective-permute-start(bf16[64,2048]{1,0:T(8,128)(2,1)} %get-tuple-element.162), channel_id=1, source_target_pairs={{0,0},{1,4},{2,8},{3,12},{4,16},{5,20},{6,24},{7,28},{8,1},{9,5},{... | collective-permute-start | bytes 786440 | tf_op jit(solution)/shard_map/ppermute | solution.py:62
  455.5 69.3 %collective-permute-start.26 = (bf16[64,2048]{1,0:T(8,128)(2,1)}, bf16[64,2048]{1,0:T(8,128)(2,1)}, u32[]{:S(2)}, u32[]{:S(2)}) collective-permute-start(bf16[64,2048]{1,0:T(8,128)(2,1)} %get-tuple-element.161), channel_id=1, source_target_pairs={{0,3},{1,7},{2,11},{3,15},{4,19},{5,23},{6,27},{7,31},{8,0},{9,4},... | collective-permute-start | bytes 786440 | tf_op jit(solution)/shard_map/ppermute | solution.py:62
  459.4 65.4 %collective-permute-start.27 = (bf16[64,2048]{1,0:T(8,128)(2,1)}, bf16[64,2048]{1,0:T(8,128)(2,1)}, u32[]{:S(2)}, u32[]{:S(2)}) collective-permute-start(bf16[64,2048]{1,0:T(8,128)(2,1)} %get-tuple-element.160), channel_id=1, source_target_pairs={{0,2},{1,6},{2,10},{3,14},{4,18},{5,22},{6,26},{7,30},{8,3},{9,7},... | collective-permute-start | bytes 786440 | tf_op jit(solution)/shard_map/ppermute | solution.py:62
  459.4 65.3 %collective-permute-start.28 = (bf16[64,2048]{1,0:T(8,128)(2,1)}, bf16[64,2048]{1,0:T(8,128)(2,1)}, u32[]{:S(2)}, u32[]{:S(2)}) collective-permute-start(bf16[64,2048]{1,0:T(8,128)(2,1)} %get-tuple-element.159), channel_id=1, source_target_pairs={{0,1},{1,5},{2,9},{3,13},{4,17},{5,21},{6,25},{7,29},{8,2},{9,6},{... | collective-permute-start | bytes 786440 | tf_op jit(solution)/shard_map/ppermute | solution.py:62
  541.4 34.3 %collective-permute-start.32 = (bf16[512,2048]{1,0:T(8,128)(2,1)}, bf16[512,2048]{1,0:T(8,128)(2,1)}, u32[]{:S(2)}, u32[]{:S(2)}) collective-permute-start(bf16[512,2048]{1,0:T(8,128)(2,1)} %convolution_convert_fusion.2), channel_id=1, source_target_pairs={{0,1},{1,0},{2,3},{3,2},{4,5},{5,4},{6,7},{7,6},{8,9},{9,8},{10,11... | collective-permute-start | bytes 6291464 | tf_op jit(solution)/shard_map/ppermute | solution.py:62
  546.8 53.3 %all-to-all-start.1 = ((bf16[32,64,384]{2,1,0:T(8,128)(2,1)}), bf16[32,64,384]{2,1,0:T(8,128)(2,1)}, u32[]{:S(2)}, u32[]{:S(2)}) async-start(bf16[32,64,384]{2,1,0:T(8,128)(2,1)} %bitcast.91), calls=%async_computation.1 | async-start | bytes 3145728 | tf_op jit(solution)/shard_map/all_to_all | solution.py:382
  (109 other events, 1517.3 us)
